TPU v7x, 32 devices: a whole 2x2x4 slice. The times are simulated.
32 devices in a mesh: dp: 2 (over core), expert: 8 (over z, y), tensor: 2 (over x).
Axes of the slice: x: 2, y: 2, z: 4, core: 2. Of those that a mesh axis runs over, the one named last changes fastest.
Arguments:
- tokens: bfloat16 [3152, 768], P(('dp', 'expert')), may hold values from -41 to 41, as said below
- ln1_scale: float32 [768], replicated, may hold values from 0.25 to 1.75
- ln1_bias: float32 [768], replicated, may hold values from -3 to 3
- w_qkv: bfloat16 [768, 3, 768], P(None, None, 'tensor'), may hold values from -0.21875 to 0.21875
- w_out: bfloat16 [768, 768], P('tensor'), may hold values from -0.875 to 0.875
- b_out: float32 [768], replicated, may hold values from -3 to 3
- ln2_scale: float32 [768], replicated, may hold values from 0.25 to 1.75
- ln2_bias: float32 [768], replicated, may hold values from -3 to 3
- w_router: bfloat16 [768, 8], replicated, may hold values from -0.09375 to 0.09375
- w_in: bfloat16 [8, 768, 3072], P('expert', None, 'tensor'), may hold values from -0.21875 to 0.21875
- b_in: float32 [8, 3072], P('expert', 'tensor'), may hold values from -3 to 3
- w_exp_out: bfloat16 [8, 3072, 768], P('expert', 'tensor'), may hold values from -1.75 to 1.75
- b_exp_out: float32 [8, 768], P('expert'), may hold values from -12 to 12
- routes: int32 [3152, 2], P(('dp', 'expert')), may hold values from 0 to 7, all different within a row
- cotangent: bfloat16 [3152, 768], P(('dp', 'expert')), may hold values from -6 to 6
Outputs:
- out: bfloat16 [3152, 768], P(('dp', 'expert'))
- grad_tokens: bfloat16 [3152, 768], P(('dp', 'expert'))
- grad_ln1_scale: float32 [768], P(('dp', 'expert'))
- grad_ln1_bias: float32 [768], P(('dp', 'expert'))
- grad_w_qkv: float32 [768, 3, 768], P(('dp', 'expert'), None, 'tensor')
- grad_w_out: float32 [768, 768], P('tensor', ('dp', 'expert'))
- grad_b_out: float32 [768], P(('dp', 'expert'))
- grad_ln2_scale: float32 [768], P(('dp', 'expert'))
- grad_ln2_bias: float32 [768], P(('dp', 'expert'))
- grad_router: float32 [768, 8], P(('dp', 'expert'))
- grad_w_in: float32 [8, 768, 3072], P('expert', None, 'tensor')
- grad_b_in: float32 [8, 3072], P('expert', 'tensor')
- grad_w_exp_out: float32 [8, 3072, 768], P('expert', 'tensor')
- grad_b_exp_out: float32 [8, 768], P('expert')
Inputs may be any that keep to these rules, and one draw needn't show every extreme that they name: `routes`: each token names two different experts, and every expert is named by some token. `tokens`: real values of varied scale.
All inputs are finite; a program needn't handle non-finite values.
Results may differ from a plain program's by a relative error of at most 0.014.
Values may be sent and summed in bfloat16 or wider, within the bound.
No kernel may reach another device: no remote copies, remote signals or barrier semaphores. Data moves between devices by JAX's collectives and lax.ppermute only.
A program may use at most 128 MiB of HBM per device.

v0:
```python
import functools

import jax
import jax.numpy as jnp
from jax import lax
from jax.experimental import pallas as pl
from jax.experimental.pallas import tpu as pltpu
from jax.sharding import PartitionSpec as P


HEAD_DIM = 64
EPSILON = 1e-06
BF = jnp.bfloat16
F32 = jnp.float32
I32 = jnp.int32
LANES = 128
SCALING = HEAD_DIM ** (-0.5)

PARAMS = pltpu.CompilerParams(vmem_limit_bytes=60 * 1024 * 1024)


def round_up(value, step):
    return -(-value // step) * step


def layer_norm(values, scale, shift):
    mean_val = jnp.mean(values, axis=-1, keepdims=True)
    centred = values - mean_val
    inv_std = lax.rsqrt(jnp.mean(centred * centred, axis=-1, keepdims=True) + EPSILON)
    x_hat = centred * inv_std
    return (x_hat * scale + shift, x_hat, inv_std)


def norm_back(grad, x_hat, inv_std, scale):
    scaled = grad * scale
    return inv_std * (
        scaled
        - jnp.mean(scaled, axis=-1, keepdims=True)
        - x_hat * jnp.mean(scaled * x_hat, axis=-1, keepdims=True)
    )


def dot32(a, b):
    return jnp.dot(a, b, preferred_element_type=F32)


def dot_nt(a, b):
    return lax.dot_general(a, b, (((1,), (1,)), ((), ())), preferred_element_type=F32)


def dot_tn(a, b):
    return lax.dot_general(a, b, (((0,), (0,)), ((), ())), preferred_element_type=F32)


def iota(shape, dim):
    return lax.broadcasted_iota(I32, shape, dim)


def gelu_both(u):
    c0 = 0.7978845608028654
    square = u * u
    th = jnp.tanh(u * (c0 + (0.044715 * c0) * square))
    half = 0.5 + 0.5 * th
    value = u * half
    slope = half + value * (1.0 - th) * (c0 + (3.0 * 0.044715 * c0) * square)
    return value, slope


def lane_slot(cap_pad):
    lane = iota((cap_pad, LANES), 1)
    slot = iota((cap_pad, LANES), 0)
    match = (lane % cap_pad == slot) & (lane < 2 * cap_pad)
    return match, lane < cap_pad


def with_pad_row(first, column, capacity):
    cap_pad = first.shape[0]
    match, is_high = lane_slot(cap_pad)
    spread = jnp.sum(jnp.where(match, column, 0.0), axis=0, keepdims=True)
    high = spread.astype(BF).astype(F32)
    value = jnp.where(is_high, high, spread - high)
    return jnp.where(iota((cap_pad, LANES), 0) == capacity, value, first)


def from_pad_row(first, capacity):
    cap_pad = first.shape[0]
    match, _ = lane_slot(cap_pad)
    row = jnp.sum(
        jnp.where(iota((cap_pad, LANES), 0) == capacity, first, 0.0), axis=0, keepdims=True
    )
    return jnp.sum(jnp.where(match, row, 0.0), axis=1, keepdims=True)


def row(ref):
    return ref[...].reshape(1, -1)


def route_kernel(sizes, ids_ref, routes_ref, cot_ref, target_ref, buffer_ref):
    rows, experts, capacity, cap_pad = sizes
    slots = experts * cap_pad
    me = ids_ref[0]
    r0, r1 = routes_ref[0:1, :], routes_ref[1:2, :]
    ids = iota((experts, rows), 0)
    hot0 = jnp.where(r0 == ids, 1.0, 0.0)
    hot1 = jnp.where(r1 == ids, 1.0, 0.0)
    before = jnp.where(iota((rows, rows), 0) < iota((rows, rows), 1), 1.0, 0.0).astype(BF)
    earlier0 = dot32(hot0.astype(BF), before)
    earlier1 = dot32(hot1.astype(BF), before) + jnp.sum(hot0, axis=1, keepdims=True)
    slot0 = jnp.sum(earlier0 * hot0, axis=0, keepdims=True).astype(I32)
    slot1 = jnp.sum(earlier1 * hot1, axis=0, keepdims=True).astype(I32)
    a0 = jnp.where(slot0 < capacity, r0 * cap_pad + slot0, slots)
    a1 = jnp.where(slot1 < capacity, r1 * cap_pad + slot1, slots)
    target_ref[...] = jnp.full(target_ref.shape, slots, I32)
    target_ref[0:1, 0:rows] = a0
    target_ref[1:2, 0:rows] = a1
    target_ref[2:3, 0:rows] = jnp.where(slot0 < capacity, (r0 ^ me) * cap_pad + slot0, slots)
    target_ref[3:4, 0:rows] = jnp.where(slot1 < capacity, (r1 ^ me) * cap_pad + slot1, slots)
    ids = iota((slots, rows), 0)
    place = jnp.where((ids == a0) | (ids == a1), 1.0, 0.0).astype(BF)
    buffer_ref[...] = dot32(place, cot_ref[...]).astype(BF)


def attention_kernel(
    tok_ref, scale_ref, shift_ref, w_ref, w_out_ref, part_ref, att_ref, qkv_ref, lse_ref
):
    normed, _, _ = layer_norm(tok_ref[...].astype(F32), row(scale_ref), row(shift_ref))
    normed = normed.astype(BF)
    rows, hidden = att_ref.shape
    for c in range(3):
        qkv_ref[c] = dot32(normed, w_ref[c]).astype(BF)
    low = iota((rows, LANES), 1) < HEAD_DIM
    for pair in range(hidden // LANES):
        cols = slice(pair * LANES, (pair + 1) * LANES)
        q, k, v = qkv_ref[0, :, cols], qkv_ref[1, :, cols], qkv_ref[2, :, cols]
        outs = []
        for part in range(2):
            mine = low if part == 0 else jnp.logical_not(low)
            scores = dot_nt(jnp.where(mine, q, jnp.zeros_like(q)), k) * SCALING
            log_sum = jnp.log(jnp.sum(jnp.exp(scores), axis=1, keepdims=True))
            weights = jnp.exp(scores - log_sum).astype(BF)
            outs.append(dot32(weights, v))
            head = 2 * pair + part
            lse_ref[:, head : head + 1] = log_sum
        att_ref[:, cols] = jnp.where(low, outs[0], outs[1]).astype(BF)
    part_ref[...] = dot32(att_ref[...], w_out_ref[...]).astype(BF)


def middle_kernel(
    sizes,
    tok_ref,
    part_ref,
    part2_ref,
    bias_ref,
    scale_ref,
    shift_ref,
    router_ref,
    routes_ref,
    target_ref,
    mixed_ref,
    probs_ref,
    *block_refs,
):
    rows, experts, capacity, cap_pad = sizes
    slots = experts * cap_pad
    mixed = (
        tok_ref[...].astype(F32)
        + (part_ref[...].astype(F32) + part2_ref[...].astype(F32))
        + row(bias_ref)
    )
    mixed_ref[...] = mixed
    normed, _, _ = layer_norm(mixed, row(scale_ref), row(shift_ref))
    normed = normed.astype(BF)
    exp_logits = jnp.exp(dot_nt(router_ref[...], normed))
    probs = exp_logits / jnp.sum(exp_logits, axis=0, keepdims=True)
    probs_ref[...] = probs
    ids = iota((experts, rows), 0)
    gate0 = jnp.sum(jnp.where(routes_ref[0:1, :] == ids, probs, 0.0), axis=0, keepdims=True)
    gate1 = jnp.sum(jnp.where(routes_ref[1:2, :] == ids, probs, 0.0), axis=0, keepdims=True)
    ids = iota((slots, rows), 0)
    in0 = ids == target_ref[2:3, 0:rows]
    in1 = ids == target_ref[3:4, 0:rows]
    gates = jnp.sum(jnp.where(in0, gate0, jnp.where(in1, gate1, 0.0)), axis=1, keepdims=True)
    place = jnp.where(in0 | in1, 1.0, 0.0).astype(BF)
    for k in range(experts):
        span = slice(k * cap_pad, (k + 1) * cap_pad)
        block = dot32(place[span], normed)
        block_refs[k][:, LANES:] = block[:, LANES:].astype(BF)
        block_refs[k][:, :LANES] = with_pad_row(block[:, :LANES], gates[span], capacity).astype(BF)


def expert_kernel(sizes, ids_ref, raw_ref, cot_ref, bias2_ref, w_ref, b_ref, *refs):
    blocks, capacity, cap_pad, held, base = sizes
    row_refs = refs[:blocks]
    x_ref, gate_ref, hidden_ref, pre_ref, bsum_ref = refs[blocks + held : blocks + held + 5]
    back_refs = refs[blocks + held + 5 : 2 * blocks + held + 5]
    acc_ref, sg_ref = refs[2 * blocks + held + 5 :]
    step, last = pl.program_id(0), pl.num_programs(0) - 1

    @pl.when(step == 0)
    def _():
        acc_ref[...] = jnp.zeros_like(acc_ref)
        first = jnp.where(ids_ref[1] == 0, 1.0, 0.0)
        for k in range(blocks):
            span = slice(k * cap_pad, (k + 1) * cap_pad)
            x_ref[span, :] = row_refs[k][...]
            gate = from_pad_row(row_refs[k][:, :LANES].astype(F32), capacity)
            gate_ref[span, :] = jnp.broadcast_to(gate, (cap_pad, LANES))
            cot = cot_ref[(base + k) ^ ids_ref[0]].astype(F32)
            side = jnp.sum(cot * bias2_ref[...], axis=1, keepdims=True)
            sg_ref[span, :] = jnp.broadcast_to(first * side, (cap_pad, LANES))

    w = w_ref[...]
    pre_act = dot32(x_ref[...], w) + b_ref[...]
    total = jnp.zeros(b_ref.shape, F32)
    for k in range(blocks):
        span = slice(k * cap_pad, (k + 1) * cap_pad)
        value, slope = gelu_both(pre_act[span])
        raw = raw_ref[(base + k) ^ ids_ref[0]]
        hidden_ref[span, :] = value.astype(BF)
        grad = gate_ref[span, 0:1] * raw * slope
        pre_ref[span, :] = grad.astype(BF)
        total = total + jnp.sum(grad, axis=0, keepdims=True)
        side = jnp.sum(value * raw, axis=1, keepdims=True)
        sg_ref[span, :] = sg_ref[span, :] + jnp.broadcast_to(side, (cap_pad, LANES))
    bsum_ref[...] = total
    acc_ref[...] += dot_nt(pre_ref[...], w)

    @pl.when(step == last)
    def _():
        for k in range(blocks):
            span = slice(k * cap_pad, (k + 1) * cap_pad)
            back_refs[k][:, LANES:] = acc_ref[span, LANES:].astype(BF)
            first = with_pad_row(acc_ref[span, :LANES], sg_ref[span, 0:1], capacity)
            back_refs[k][:, :LANES] = first.astype(BF)


def expert_out_kernel(
    sizes, ids_ref, gate_ref, cot_ref, bias2_ref, hidden_ref, w_ref, out_ref, sent_ref, bsum_ref, acc_ref
):
    experts, _, cap_pad = sizes
    step, last = pl.program_id(0), pl.num_programs(0) - 1

    @pl.when(step == 0)
    def _():
        acc_ref[...] = jnp.zeros_like(acc_ref)
        total = jnp.zeros(bsum_ref.shape, F32)
        for k in range(experts):
            span = slice(k * cap_pad, (k + 1) * cap_pad)
            sent = gate_ref[span, 0:1] * cot_ref[k ^ ids_ref[0]].astype(F32)
            total = total + jnp.sum(sent, axis=0, keepdims=True)
            sent_ref[span, :] = sent.astype(BF)
        bsum_ref[...] = total

    acc_ref[...] += dot32(hidden_ref[...], w_ref[...])

    @pl.when(step == last)
    def _():
        bias = jnp.where(ids_ref[1] == 0, 1.0, 0.0) * bias2_ref[...]
        for k in range(experts):
            span = slice(k * cap_pad, (k + 1) * cap_pad)
            value = gate_ref[span, 0:1] * (acc_ref[span, :] + bias)
            out_ref[k ^ ids_ref[0]] = value.astype(BF)


def combine_kernel(sizes, target_ref, *refs):
    _, experts, capacity, cap_pad = sizes
    block_refs, (pack_ref, x_ref) = refs[:experts], refs[experts:]
    slots = experts * cap_pad
    lanes = target_ref.shape[1]
    body = pack_ref.shape[0] - 16
    gg0 = jnp.zeros((1, lanes), F32)
    gg1 = jnp.zeros((1, lanes), F32)
    for k in range(experts):
        span = slice(k * cap_pad, (k + 1) * cap_pad)
        x_ref[span, :] = block_refs[k][...]
        side = from_pad_row(block_refs[k][:, :LANES].astype(F32), capacity)
        ids = iota((cap_pad, lanes), 0) + k * cap_pad
        gg0 += jnp.sum(jnp.where(ids == target_ref[2:3, :], side, 0.0), axis=0, keepdims=True)
        gg1 += jnp.sum(jnp.where(ids == target_ref[3:4, :], side, 0.0), axis=0, keepdims=True)
    ids = iota((slots, lanes), 0)
    place = jnp.where(
        (ids == target_ref[2:3, :]) | (ids == target_ref[3:4, :]), 1.0, 0.0
    ).astype(BF)
    part = dot_tn(place, x_ref[...])
    pack_ref[0:body, :] = part[0:body].astype(BF)
    pack_ref[body:, :] = jnp.zeros((16, pack_ref.shape[1]), BF)
    line = iota((16, lanes), 0)
    high0, high1 = gg0.astype(BF).astype(F32), gg1.astype(BF).astype(F32)
    tail = jnp.where(line == 0, high0, jnp.where(line == 1, gg0 - high0, 0.0))
    tail = jnp.where(line == 2, high1, jnp.where(line == 3, gg1 - high1, tail))
    pack_ref[body:, 0:lanes] = tail.astype(BF)


def gather_out_kernel(sizes, target_ref, x_ref, out_ref):
    _, experts, _, cap_pad = sizes
    ids = iota((experts * cap_pad, target_ref.shape[1]), 0)
    place = jnp.where(
        (ids == target_ref[0:1, :]) | (ids == target_ref[1:2, :]), 1.0, 0.0
    ).astype(BF)
    out_ref[...] = dot_tn(place, x_ref[...])[0 : out_ref.shape[0]].astype(BF)


def halves(ids_ref, width):
    half = width // 2
    return (
        pl.ds(pl.multiple_of(ids_ref[2] * half, LANES), half),
        pl.ds(pl.multiple_of((1 - ids_ref[2]) * half, LANES), half),
    )


def norm2_back_kernel(
    sizes,
    ids_ref,
    pack_ref,
    pack2_ref,
    mixed_ref,
    probs_ref,
    routes_ref,
    router_ref,
    cot_ref,
    scale_ref,
    shift_ref,
    att_ref,
    w_out_ref,
    qkv_ref,
    lse_ref,
    tok_ref,
    scale1_ref,
    shift1_ref,
    grad_ref,
    grad_att_ref,
    grad_v_ref,
    keep_ref,
    send_ref,
    small_ref,
    left_ref,
):
    rows, experts, _, _ = sizes
    width = tok_ref.shape[1]
    hidden = att_ref.shape[1]
    body = pack_ref.shape[0] - 16
    tail = pack_ref[body:, 0:rows].astype(F32) + pack2_ref[body:, 0:rows].astype(F32)
    gg0 = tail[0:1] + tail[1:2]
    gg1 = tail[2:3] + tail[3:4]
    ids = iota((experts, rows), 0)
    grad_probs = jnp.where(routes_ref[0:1, :] == ids, gg0, 0.0) + jnp.where(
        routes_ref[1:2, :] == ids, gg1, 0.0
    )
    probs = probs_ref[...]
    grad_logits = probs * (grad_probs - jnp.sum(probs * grad_probs, axis=0, keepdims=True))
    grad_logits = grad_logits.astype(BF)
    grad_normed = (
        pack_ref[0:rows, :].astype(F32)
        + pack2_ref[0:rows, :].astype(F32)
        + dot_tn(grad_logits, router_ref[...])
    )
    normed, x_hat, inv_std = layer_norm(mixed_ref[...], row(scale_ref), row(shift_ref))
    grad_mixed = cot_ref[...].astype(F32) + norm_back(grad_normed, x_hat, inv_std, row(scale_ref))
    grad_ref[...] = grad_mixed
    left_ref[...] = grad_mixed.astype(BF)
    sides = tuple(zip((keep_ref, send_ref), halves(ids_ref, width)))
    for ref, cols in sides:
        ref[:, 0:hidden] = dot_tn(left_ref[:, cols], att_ref[...]).astype(BF)
    small_ref[...] = jnp.zeros_like(small_ref)
    small_ref[0:experts, :] = dot32(grad_logits, normed.astype(BF))
    small_ref[experts : experts + 1, :] = jnp.sum(grad_mixed, axis=0, keepdims=True)
    small_ref[experts + 1 : experts + 2, :] = jnp.sum(grad_normed * x_hat, axis=0, keepdims=True)
    small_ref[experts + 2 : experts + 3, :] = jnp.sum(grad_normed, axis=0, keepdims=True)
    for ref, cols in sides:
        ref[:, 2 * hidden :] = small_ref[:, cols].T.astype(BF)
    grad_att_ref[...] = dot_nt(left_ref[...], w_out_ref[...]).astype(BF)
    low = iota((rows, LANES), 1) < HEAD_DIM
    for pair in range(hidden // LANES):
        cols = slice(pair * LANES, (pair + 1) * LANES)
        q, k = qkv_ref[0, :, cols], qkv_ref[1, :, cols]
        g = grad_att_ref[:, cols]
        outs = []
        for part in range(2):
            mine = low if part == 0 else jnp.logical_not(low)
            head = 2 * pair + part
            scores = dot_nt(jnp.where(mine, q, jnp.zeros_like(q)), k) * SCALING
            weights = jnp.exp(scores - lse_ref[:, head : head + 1])
            outs.append(dot_tn(weights.astype(BF), g))
        grad_v_ref[:, cols] = jnp.where(low, outs[0], outs[1]).astype(BF)
    normed1, _, _ = layer_norm(tok_ref[...].astype(F32), row(scale1_ref), row(shift1_ref))
    left_ref[...] = normed1.astype(BF)
    for ref, cols in sides:
        ref[:, hidden : 2 * hidden] = dot_tn(left_ref[:, cols], grad_v_ref[...]).astype(BF)


def attention_back_kernel(
    ids_ref,
    grad_att_ref,
    grad_v_ref,
    qkv_ref,
    lse_ref,
    tok_ref,
    scale_ref,
    shift_ref,
    w_ref,
    part_ref,
    keep_ref,
    send_ref,
    gqk_ref,
    small_ref,
    left_ref,
):
    rows, width = tok_ref.shape
    hidden = grad_att_ref.shape[1]
    low = iota((rows, LANES), 1) < HEAD_DIM
    for pair in range(hidden // LANES):
        cols = slice(pair * LANES, (pair + 1) * LANES)
        q, k, v = qkv_ref[0, :, cols], qkv_ref[1, :, cols], qkv_ref[2, :, cols]
        g = grad_att_ref[:, cols]
        outs = []
        for part in range(2):
            mine = low if part == 0 else jnp.logical_not(low)
            head = 2 * pair + part
            scores = dot_nt(jnp.where(mine, q, jnp.zeros_like(q)), k) * SCALING
            weights = jnp.exp(scores - lse_ref[:, head : head + 1])
            grad_w = dot_nt(jnp.where(mine, g, jnp.zeros_like(g)), v)
            delta = jnp.sum(weights * grad_w, axis=1, keepdims=True)
            grad_s = (weights * (grad_w - delta) * SCALING).astype(BF)
            outs.append((dot32(grad_s, k), dot_tn(grad_s, q)))
        for c in range(2):
            gqk_ref[c, :, cols] = jnp.where(low, outs[0][c], outs[1][c]).astype(BF)
    part = dot_nt(gqk_ref[0], w_ref[0]) + dot_nt(gqk_ref[1], w_ref[1]) + dot_nt(grad_v_ref[...], w_ref[2])
    part_ref[...] = part.astype(BF)
    normed, x_hat, _ = layer_norm(tok_ref[...].astype(F32), row(scale_ref), row(shift_ref))
    left_ref[...] = normed.astype(BF)
    small_ref[...] = jnp.zeros_like(small_ref)
    small_ref[0:1, :] = jnp.sum(part * x_hat, axis=0, keepdims=True)
    small_ref[1:2, :] = jnp.sum(part, axis=0, keepdims=True)
    for ref, cols in zip((keep_ref, send_ref), halves(ids_ref, width)):
        for c in range(2):
            ref[:, c * hidden : (c + 1) * hidden] = dot_tn(left_ref[:, cols], gqk_ref[c]).astype(BF)
        ref[:, 2 * hidden :] = small_ref[:, cols].T.astype(BF)


def norm1_back_kernel(part_ref, part2_ref, tok_ref, scale_ref, shift_ref, grad_ref, out_ref):
    grad = part_ref[...].astype(F32) + part2_ref[...].astype(F32)
    _, x_hat, inv_std = layer_norm(tok_ref[...].astype(F32), row(scale_ref), row(shift_ref))
    out_ref[...] = (grad_ref[...] + norm_back(grad, x_hat, inv_std, row(scale_ref))).astype(BF)


def hop_kernel(bit, ids_ref, kept_ref, got_ref, keep_ref, send_ref):
    mine = (ids_ref[0] >> bit) & 1
    for j in range(keep_ref.shape[0]):
        a, b = 2 * j + mine, 2 * j + 1 - mine
        keep_ref[j] = (kept_ref[a].astype(F32) + got_ref[a].astype(F32)).astype(BF)
        send_ref[j] = (kept_ref[b].astype(F32) + got_ref[b].astype(F32)).astype(BF)


def early_end_kernel(part_ref, w_out_ref, v_ref, small_ref):
    hidden = v_ref.shape[1]
    total = part_ref[0].astype(F32)
    for k in range(1, part_ref.shape[0]):
        total = total + part_ref[k].astype(F32)
    w_out_ref[...] = total[:, :hidden]
    v_ref[...] = total[:, hidden : 2 * hidden]
    small_ref[...] = total[:, 2 * hidden :]


def late_end_kernel(kept_ref, got_ref, v_ref, qkv_ref, ln1_ref):
    hidden = v_ref.shape[1]
    total = kept_ref[0].astype(F32) + got_ref[0].astype(F32)
    qkv_ref[0] = total[:, :hidden]
    qkv_ref[1] = total[:, hidden : 2 * hidden]
    qkv_ref[2] = v_ref[...]
    ln1_ref[...] = total[:, 2 * hidden :]


def weight_grad_kernel(ids_ref, a_ref, a2_ref, b_ref, b2_ref, out_ref):
    @pl.when(ids_ref[2] == 0)
    def _():
        out_ref[...] = dot_tn(a_ref[...], b_ref[...]) + dot_tn(a2_ref[...], b2_ref[...])

    @pl.when(ids_ref[2] == 1)
    def _():
        out_ref[...] = dot_tn(a2_ref[...], b2_ref[...]) + dot_tn(a_ref[...], b_ref[...])


def weight_grad(ids, a, a2, b, b2):
    slots, rows = a.shape
    cols = b.shape[1]
    tile = 512 if rows % 512 == 0 and rows > cols else 256
    left = pl.BlockSpec((slots, tile), lambda i: (0, i))
    right = pl.BlockSpec((slots, cols), lambda i: (0, 0))
    return pl.pallas_call(
        weight_grad_kernel,
        grid=(rows // tile,),
        out_shape=jax.ShapeDtypeStruct((rows, cols), F32),
        in_specs=[pl.BlockSpec(memory_space=pltpu.SMEM), left, left, right, right],
        out_specs=pl.BlockSpec((tile, cols), lambda i: (i, 0)),
        compiler_params=PARAMS,
        cost_estimate=pl.CostEstimate(
            flops=4 * slots * rows * cols, bytes_accessed=9_000_000, transcendentals=0
        ),
    )(ids, a, a2, b, b2)


def call(kernel, outs, *args, scratch=(), scalars=0, flops=0):
    specs = [
        pl.BlockSpec(memory_space=pltpu.SMEM if i < scalars else pltpu.VMEM)
        for i in range(len(args))
    ]
    moved = sum(a.size * a.dtype.itemsize for a in args)
    return pl.pallas_call(
        kernel,
        out_shape=tuple(jax.ShapeDtypeStruct(s, d) for s, d in outs),
        in_specs=specs,
        out_specs=tuple(pl.BlockSpec(memory_space=pltpu.VMEM) for _ in outs),
        scratch_shapes=list(scratch),
        compiler_params=PARAMS,
        cost_estimate=pl.CostEstimate(flops=flops, bytes_accessed=moved, transcendentals=0),
    )(*args)


def swap(x, axis):
    return lax.ppermute(x, axis, [(0, 1), (1, 0)])


def xor_exchange(blocks, count, order):
    outs = {}
    for k in order:
        outs[k] = lax.ppermute(blocks[k], "expert", [(i, i ^ k) for i in range(count)])
    return outs


def all_to_all(x):
    return lax.all_to_all(x, "expert", split_axis=0, concat_axis=0, tiled=True)


def reduce_dense(ids, keep, send):
    count = lax.axis_size("expert")
    piece = keep.shape[0] // count
    cols = keep.shape[1]
    got = swap(send, "dp").reshape(count, piece, cols)
    keep = keep.reshape(count, piece, cols)
    bit, left = 0, count
    while left > 1:
        left //= 2
        keep, send = call(
            functools.partial(hop_kernel, bit),
            [((left, piece, cols), BF), ((left, piece, cols), BF)],
            ids, keep, got,
            scalars=1,
        )
        got = lax.ppermute(send, "expert", [(i, i ^ (1 << bit)) for i in range(count)])
        bit += 1
    return keep, got


def per_device(
    tokens,
    ln1_scale,
    ln1_bias,
    w_qkv,
    w_out,
    b_out,
    ln2_scale,
    ln2_bias,
    w_router,
    w_in,
    b_in,
    w_exp_out,
    b_exp_out,
    routes,
    cotangent,
):
    rows, width = tokens.shape
    experts = w_router.shape[1]
    count = lax.axis_size("expert")
    ids = jnp.stack(
        [lax.axis_index("expert"), lax.axis_index("tensor"), lax.axis_index("dp")]
    ).astype(I32)
    capacity = (5 * rows + 2 * experts - 1) // (2 * experts)
    cap_pad = round_up(capacity + 1, 16)
    slots = experts * cap_pad
    hidden = w_qkv.shape[2]
    inner = w_in.shape[2]
    lanes = round_up(rows, LANES)
    half = width // 2
    sizes = (rows, experts, capacity, cap_pad)
    w_in, w_exp_out = w_in[0], w_exp_out[0]
    w3 = w_qkv.transpose(1, 0, 2)
    router_t = w_router.T
    routes_t = routes.T

    target, cot_buffer = call(
        functools.partial(route_kernel, sizes),
        [((4, lanes), I32), ((slots, width), BF)],
        ids, routes_t, cotangent,
        scalars=1, flops=2 * slots * rows * width,
    )
    cot_rows = all_to_all(cot_buffer.reshape(experts, cap_pad, width))
    part, attended, qkv, lse = call(
        attention_kernel,
        [((rows, width), BF), ((rows, hidden), BF), ((3, rows, hidden), BF), ((rows, LANES), F32)],
        tokens, ln1_scale, ln1_bias, w3, w_out,
        flops=8 * rows * width * hidden,
    )
    part_other = swap(part, "tensor")
    mixed, probs, *blocks = call(
        functools.partial(middle_kernel, sizes),
        [((rows, width), F32), ((experts, rows), F32)] + [((cap_pad, width), BF)] * experts,
        tokens, part, part_other, b_out, ln2_scale, ln2_bias, router_t, routes_t, target,
        flops=2 * slots * rows * width,
    )
    near = experts
    order = tuple(range(experts - 1, 0, -1))
    received = xor_exchange(blocks, count, order)
    received[0] = blocks[0]

    tile = 384
    grid = inner // tile
    whole = lambda shape: pl.BlockSpec(shape, lambda f: (0,) * len(shape))
    smem = pl.BlockSpec(memory_space=pltpu.SMEM)
    anywhere = pl.BlockSpec(memory_space=pl.ANY)
    raw = dot_nt(cot_rows.reshape(slots, width), w_exp_out).reshape(experts, cap_pad, inner)

    def expert(which, held):
        span = near * cap_pad
        at = lambda f: (which, f)
        fixed = lambda f: (which, 0)
        shapes = [
            jax.ShapeDtypeStruct((slots, width), BF),
            jax.ShapeDtypeStruct((slots, LANES), F32),
            jax.ShapeDtypeStruct((slots, inner), BF),
            jax.ShapeDtypeStruct((slots, inner), BF),
        ]
        return pl.pallas_call(
            functools.partial(expert_kernel, (near, capacity, cap_pad, len(held), which * near)),
            grid=(grid,),
            out_shape=shapes
            + [jax.ShapeDtypeStruct((1, inner), F32)]
            + [jax.ShapeDtypeStruct((cap_pad, width), BF)] * near,
            in_specs=[
                smem,
                pl.BlockSpec((experts, cap_pad, tile), lambda f: (0, 0, f)),
                whole((experts, cap_pad, width)),
                whole((1, width)),
                pl.BlockSpec((width, tile), lambda f: (0, f)),
                pl.BlockSpec((1, tile), lambda f: (0, f)),
            ]
            + [whole((cap_pad, width))] * near
            + [anywhere] * len(held),
            out_specs=[
                pl.BlockSpec((span, width), fixed),
                pl.BlockSpec((span, LANES), fixed),
                pl.BlockSpec((span, tile), at),
                pl.BlockSpec((span, tile), at),
                pl.BlockSpec((1, tile), lambda f: (0, f)),
            ]
            + [whole((cap_pad, width))] * near,
            input_output_aliases={6 + near + i: i for i in range(len(held))},
            scratch_shapes=[pltpu.VMEM((span, width), F32), pltpu.VMEM((span, LANES), F32)],
            compiler_params=PARAMS,
            cost_estimate=pl.CostEstimate(
                flops=2 * slots * width * inner, bytes_accessed=6_000_000, transcendentals=0
            ),
        )(
            ids, raw, cot_rows, b_exp_out, w_in, b_in,
            *[received[which * near + i] for i in range(near)],
            *held,
        )

    outs = expert(0, ())
    x_rows, gate, hidden_act, grad_pre, grad_b1 = outs[:5]
    back = xor_exchange(outs[5:], count, order)
    back[0] = outs[5]
    out_rows, grad_sent, grad_b2 = pl.pallas_call(
        functools.partial(expert_out_kernel, (experts, capacity, cap_pad)),
        grid=(grid,),
        out_shape=[
            jax.ShapeDtypeStruct((experts, cap_pad, width), BF),
            jax.ShapeDtypeStruct((slots, width), BF),
            jax.ShapeDtypeStruct((1, width), F32),
        ],
        in_specs=[
            smem,
            whole((slots, LANES)),
            whole((experts, cap_pad, width)),
            whole((1, width)),
            pl.BlockSpec((slots, tile), lambda f: (0, f)),
            pl.BlockSpec((tile, width), lambda f: (f, 0)),
        ],
        out_specs=[whole((experts, cap_pad, width)), whole((slots, width)), whole((1, width))],
        scratch_shapes=[pltpu.VMEM((slots, width), F32)],
        compiler_params=PARAMS,
        cost_estimate=pl.CostEstimate(
            flops=2 * slots * width * inner, bytes_accessed=6_000_000, transcendentals=0
        ),
        name="expert_out",
    )(ids, gate, cot_rows, b_exp_out, hidden_act, w_exp_out)
    x_other = swap(x_rows, "dp")
    pre_other = swap(grad_pre, "dp")
    hidden_other = swap(hidden_act, "dp")
    sent_other = swap(grad_sent, "dp")
    grad_w_in = weight_grad(ids, x_rows, x_other, grad_pre, pre_other)
    grad_w_exp_out = weight_grad(ids, hidden_act, hidden_other, grad_sent, sent_other)
    biases = jnp.concatenate([grad_b1, grad_b2], axis=1)
    biases = biases + swap(biases, "dp")
    body = round_up(rows, 16)
    target, out_rows = lax.optimization_barrier((target, out_rows))
    (pack,) = call(
        functools.partial(combine_kernel, sizes),
        [((body + 16, width), BF)],
        target, *[back[k] for k in range(experts)],
        scratch=[pltpu.VMEM((slots, width), BF)],
        flops=2 * slots * rows * width,
    )
    pack_other = swap(pack, "tensor")
    out_rows, pack = lax.optimization_barrier((out_rows, pack))
    out_back = all_to_all(out_rows)
    grad_mixed, grad_att, grad_v, keep, send = call(
        functools.partial(norm2_back_kernel, sizes),
        [
            ((rows, width), F32),
            ((rows, hidden), BF),
            ((rows, hidden), BF),
            ((half, 2 * hidden + LANES), BF),
            ((half, 2 * hidden + LANES), BF),
        ],
        ids, pack, pack_other, mixed, probs, routes_t, router_t, cotangent, ln2_scale,
        ln2_bias, attended, w_out, qkv, lse, tokens, ln1_scale, ln1_bias,
        scratch=[pltpu.VMEM((LANES, width), F32), pltpu.VMEM((rows, width), BF)],
        scalars=1, flops=8 * rows * width * hidden,
    )
    piece = half // count
    got = swap(send, "dp")
    early = (keep.astype(F32) + got.astype(F32)).astype(BF)
    early = all_to_all(early.reshape(count, piece, -1))
    part1, keep, send = call(
        attention_back_kernel,
        [((rows, width), BF), ((half, 2 * hidden + LANES), BF), ((half, 2 * hidden + LANES), BF)],
        ids, grad_att, grad_v, qkv, lse, tokens, ln1_scale, ln1_bias, w3,
        scratch=[
            pltpu.VMEM((2, rows, hidden), BF),
            pltpu.VMEM((LANES, width), F32),
            pltpu.VMEM((rows, width), BF),
        ],
        scalars=1, flops=12 * rows * width * hidden,
    )
    late = reduce_dense(ids, keep, send)
    part1_other = swap(part1, "tensor")
    w_out_t, grad_v_w, small = call(
        early_end_kernel,
        [((piece, hidden), F32), ((piece, hidden), F32), ((piece, LANES), F32)],
        early,
    )
    grad_w_qkv, ln1 = call(
        late_end_kernel,
        [((3, piece, hidden), F32), ((piece, LANES), F32)],
        *late, grad_v_w,
    )
    ln1 = ln1 + swap(ln1, "tensor")
    (grad_tokens,) = call(
        norm1_back_kernel,
        [((rows, width), BF)],
        part1, part1_other, tokens, ln1_scale, ln1_bias, grad_mixed,
    )
    (out_part,) = call(
        functools.partial(gather_out_kernel, sizes),
        [((rows, width), BF)],
        target, out_back.reshape(slots, width),
        flops=2 * slots * rows * width,
    )
    out_other = swap(out_part, "tensor")
    out = (mixed + (out_part.astype(F32) + out_other.astype(F32))).astype(BF)
    return (
        out,
        grad_tokens,
        ln1[:, 0],
        ln1[:, 1],
        grad_w_qkv.transpose(1, 0, 2),
        w_out_t.T,
        small[:, experts],
        small[:, experts + 1],
        small[:, experts + 2],
        small[:, :experts],
        grad_w_in[None],
        biases[:, :inner],
        grad_w_exp_out[None],
        biases[:, inner:],
    )


def solution(mesh):
    rows = P(("dp", "expert"), None)
    shard = P(("dp", "expert"))
    placed = (
        rows,
        P(),
        P(),
        P(None, None, "tensor"),
        P("tensor", None),
        P(),
        P(),
        P(),
        P(),
        P("expert", None, "tensor"),
        P("expert", "tensor"),
        P("expert", "tensor", None),
        P("expert", None),
        rows,
        rows,
    )
    return jax.shard_map(
        per_device,
        mesh=mesh,
        in_specs=placed,
        out_specs=(
            rows,
            rows,
            shard,
            shard,
            P(("dp", "expert"), None, "tensor"),
            P("tensor", ("dp", "expert")),
            shard,
            shard,
            shard,
            rows,
            P("expert", None, "tensor"),
            P("expert", "tensor"),
            P("expert", "tensor", None),
            P("expert", None),
        ),
        check_vma=False,
    )
```

profile of v0, /device:TPU:0, one launch (start us, length us, event | category | flops | bytes accessed | tf_op | source)
XLA Modules:
  0.0 171.7 jit_solution(12288948660050285478)
XLA Ops:
  1.2 2.4 %shard_map.255 = (s32[4,256]{1,0:T(4,128)}, bf16[512,768]{1,0:T(8,128)(2,1)}) custom-call(s32[3]{0:T(128)} %pad_add_fusion.ids_ref, s32[2,197]{1,0:T(2,128)} %bitcast.35, bf16[197,768]{1,0:T(8,128)(2,1)} %cot_ref.3), custom_call_target="tpu_custom_call" | custom-call | flops 154927104 | bytes 304180 | tf_op jit(solution)/shard_map/pallas_call | solution.py:508
  3.6 7.4 %all-to-all-start = ((bf16[8,64,768]{2,1,0:T(8,128)(2,1)}), bf16[8,64,768]{2,1,0:T(8,128)(2,1)S(1)}, u32[]{:S(2)}, u32[]{:S(2)}) async-start(bf16[8,64,768]{2,1,0:T(8,128)(2,1)} %bitcast.30), calls=%async_computation | async-start | bytes 1572864 | tf_op jit(solution)/shard_map/all_to_all | solution.py:531
  11.1 4.3 %shard_map.254 = (bf16[197,768]{1,0:T(8,128)(2,1)}, bf16[197,384]{1,0:T(8,128)(2,1)}, bf16[3,197,384]{2,1,0:T(8,128)(2,1)}, f32[197,128]{1,0:T(8,128)}) custom-call(bf16[197,768]{1,0:T(8,128)(2,1)} %tok_ref.9, f32[768]{0:T(1024)} %scale_ref.9, f32[768]{0:T(1024)} %shift_ref.9, bf16[3,768,384]{2,1,0:T(8,128)(2,1)} %bitcast.22, bf16[384,768]{1,0:T(8,128)(2,1)} %w_out_ref.3), custom_call_target="tpu_custom_call" | custom-call | flops 464781312 | bytes 2668032 | tf_op jit(solution)/shard_map/pallas_call | solution.py:508
  15.3 1.5 collective-permute-start
  16.8 7.4 %collective-permute-done.part2_ref = bf16[197,768]{1,0:T(8,128)(2,1)S(1)} collective-permute-done((bf16[197,768]{1,0:T(8,128)(2,1)}, bf16[197,768]{1,0:T(8,128)(2,1)S(1)}, u32[]{:S(2)}, u32[]{:S(2)}) %collective-permute-start) | collective-permute-done | bytes 302624 | tf_op jit(solution)/shard_map/ppermute | solution.py:520
  25.0 3.2 %shard_map.256 = (f32[197,768]{1,0:T(8,128)}, f32[8,197]{1,0:T(8,128)}, bf16[64,768]{1,0:T(8,128)(2,1)}, bf16[64,768]{1,0:T(8,128)(2,1)}, bf16[64,768]{1,0:T(8,1...) custom-call(bf16[197,768]{1,0:T(8,128)(2,1)} %tok_ref.9, ...), custom_call_target="tpu_custom_call" | custom-call | flops 154927104 | bytes 934952 | tf_op jit(solution)/shard_map/pallas_call | solution.py:508
  28.1 1.7 %collective-permute-start.1 = (bf16[64,768]{1,0:T(8,128)(2,1)}, bf16[64,768]{1,0:T(8,128)(2,1)S(1)}, u32[]{:S(2)}, u32[]{:S(2)}) collective-permute-start(bf16[64,768]{1,0:T(8,128)(2,1)} %get-tuple-element.74), channel_id=1, source_target_pairs={{0,2},{2,0},{4,6},{6,4},{8,10},{10,8},{12,14},{14,12},{1,3},{3,1},... | collective-permute-start | bytes 294920 | tf_op jit(solution)/shard_map/ppermute | solution.py:526
  29.9 1.5 collective-permute-start.2
  31.6 2.6 %collective-permute-start.4 = (bf16[64,768]{1,0:T(8,128)(2,1)}, bf16[64,768]{1,0:T(8,128)(2,1)S(1)}, u32[]{:S(2)}, u32[]{:S(2)}) collective-permute-start(bf16[64,768]{1,0:T(8,128)(2,1)} %get-tuple-element.77), channel_id=1, source_target_pairs={{0,8},{2,10},{4,12},{6,14},{8,0},{10,2},{12,4},{14,6},{1,9},{3,11}... | collective-permute-start | bytes 294920 | tf_op jit(solution)/shard_map/ppermute | solution.py:526
  34.3 1.5 collective-permute-start.5
  35.7 3.3 %collective-permute-start.6 = (bf16[64,768]{1,0:T(8,128)(2,1)}, bf16[64,768]{1,0:T(8,128)(2,1)}, u32[]{:S(2)}, u32[]{:S(2)}) collective-permute-start(bf16[64,768]{1,0:T(8,128)(2,1)} %get-tuple-element.79), channel_id=1, source_target_pairs={{0,12},{2,14},{4,8},{6,10},{8,4},{10,6},{12,0},{14,2},{1,13},{3,15... | collective-permute-start | bytes 294920 | tf_op jit(solution)/shard_map/ppermute | solution.py:526
  39.3 3.1 %fusion.raw_ref = f32[8,64,1536]{2,1,0:T(8,128)} fusion(bf16[8,64,768]{2,1,0:T(8,128)(2,1)S(1)} %all-to-all-done.cot_ref, bf16[1,1536,768]{2,1,0:T(8,128)(2,1)S(1)} %copy-done.5), kind=kOutput, calls=%fused_computation | convolution fusion | flops 1207959552 | bytes 6291456 | tf_op jit(solution)/shard_map/dot_general | solution.py:48
  42.4 3.4 %collective-permute-done.4.refs_4_ = bf16[64,768]{1,0:T(8,128)(2,1)S(1)} collective-permute-done((bf16[64,768]{1,0:T(8,128)(2,1)}, bf16[64,768]{1,0:T(8,128)(2,1)S(1)}, u32[]{:S(2)}, u32[]{:S(2)}) %collective-permute-start.4) | collective-permute-done | bytes 98336 | tf_op jit(solution)/shard_map/ppermute | solution.py:526
  45.8 3.7 %collective-permute-done.5.refs_5_ = bf16[64,768]{1,0:T(8,128)(2,1)} collective-permute-done((bf16[64,768]{1,0:T(8,128)(2,1)}, bf16[64,768]{1,0:T(8,128)(2,1)}, u32[]{:S(2)}, u32[]{:S(2)}) %collective-permute-start.5) | collective-permute-done | bytes 98336 | tf_op jit(solution)/shard_map/ppermute | solution.py:526
  49.5 10.0 %shard_map.257 = (bf16[512,768]{1,0:T(8,128)(2,1)}, f32[512,128]{1,0:T(8,128)}, bf16[512,1536]{1,0:T(8,128)(2,1)}, bf16[512,1536]{1,0:T(8,128)(2,1)}, f32[1,1536...) custom-call(s32[3]{0:T(128)} %pad_add_fusion.ids_ref, ...), custom_call_target="tpu_custom_call" | custom-call | flops 1207959552 | bytes 6000000 | tf_op jit(solution)/shard_map/pallas_call | solution.py:632
  59.6 3.6 %collective-permute-start.9 = (bf16[64,768]{1,0:T(8,128)(2,1)}, bf16[64,768]{1,0:T(8,128)(2,1)S(1)}, u32[]{:S(2)}, u32[]{:S(2)}) collective-permute-start(bf16[64,768]{1,0:T(8,128)(2,1)} %get-tuple-element.88), channel_id=1, source_target_pairs={{0,4},{2,6},{4,0},{6,2},{8,12},{10,14},{12,8},{14,10},{1,5},{3,7},... | collective-permute-start | bytes 294920 | tf_op jit(solution)/shard_map/ppermute | solution.py:526
  63.2 0.9 collective-permute-start.10
  64.1 2.8 %collective-permute-start.11 = (bf16[64,768]{1,0:T(8,128)(2,1)}, bf16[64,768]{1,0:T(8,128)(2,1)S(1)}, u32[]{:S(2)}, u32[]{:S(2)}) collective-permute-start(bf16[64,768]{1,0:T(8,128)(2,1)} %get-tuple-element.90), channel_id=1, source_target_pairs={{0,8},{2,10},{4,12},{6,14},{8,0},{10,2},{12,4},{14,6},{1,9},{3,11}... | collective-permute-start | bytes 294920 | tf_op jit(solution)/shard_map/ppermute | solution.py:526
  67.0 2.3 %collective-permute-start.13 = (bf16[64,768]{1,0:T(8,128)(2,1)}, bf16[64,768]{1,0:T(8,128)(2,1)S(1)}, u32[]{:S(2)}, u32[]{:S(2)}) collective-permute-start(bf16[64,768]{1,0:T(8,128)(2,1)} %get-tuple-element.92), channel_id=1, source_target_pairs={{0,12},{2,14},{4,8},{6,10},{8,4},{10,6},{12,0},{14,2},{1,13},{3,15... | collective-permute-start | bytes 294920 | tf_op jit(solution)/shard_map/ppermute | solution.py:526
  69.3 2.4 %collective-permute-start.14 = (bf16[64,768]{1,0:T(8,128)(2,1)}, bf16[64,768]{1,0:T(8,128)(2,1)S(1)}, u32[]{:S(2)}, u32[]{:S(2)}) collective-permute-start(bf16[64,768]{1,0:T(8,128)(2,1)} %get-tuple-element.93), channel_id=1, source_target_pairs={{0,14},{2,12},{4,10},{6,8},{8,6},{10,4},{12,2},{14,0},{1,15},{3,13... | collective-permute-start | bytes 294920 | tf_op jit(solution)/shard_map/ppermute | solution.py:526
  71.8 6.3 %expert_out.1 = (bf16[8,64,768]{2,1,0:T(8,128)(2,1)}, bf16[512,768]{1,0:T(8,128)(2,1)}, f32[1,768]{1,0:T(1,128)}) custom-call(s32[3]{0:T(128)} %pad_add_fusion.ids_ref, f32[512,128]{1,0:T(8,128)} %get-tuple-element.81.gate_ref, bf16[8,64,768]{2,1,0:T(8,128)(2,1)} %copy-done, f32[1,768]{1,0:T(1,128)} %bias2_ref.3, ...), custom_call_target="tpu_custom_call" | custom-call | flops 1207959552 | bytes 6000000 | tf_op jit(solution)/shard_map/expert_out/pallas_call | solution.py:672
  78.1 2.0 %collective-permute-done.12.refs_5_ = bf16[64,768]{1,0:T(8,128)(2,1)S(1)} collective-permute-done((bf16[64,768]{1,0:T(8,128)(2,1)}, bf16[64,768]{1,0:T(8,128)(2,1)S(1)}, u32[]{:S(2)}, u32[]{:S(2)}) %collective-permute-start.12) | collective-permute-done | bytes 98336 | tf_op jit(solution)/shard_map/ppermute | solution.py:526
  80.8 2.4 %shard_map.258.pack_ref = bf16[224,768]{1,0:T(8,128)(2,1)} custom-call(s32[4,256]{1,0:T(4,128)} %get-tuple-element.84.target_ref, bf16[64,768]{1,0:T(8,128)(2,1)} %get-tuple-element.86.refs_0_, bf16[64,768]{1,0:T(8,128)(2,1)} %copy-done.13, bf16[64,768]{1,0:T(8,128)(2,1)} %copy-done.14, bf16[64,768]{1,0:T(8,128)(2,1)} %copy-done.15, ...), custom_call_target="tpu_custom_call" | custom-call | flops 154927104 | bytes 790528 | tf_op jit(solution)/shard_map/pallas_call | solution.py:508
  83.2 1.5 collective-permute-start.16
  84.7 6.2 %all-to-all-start.1 = ((bf16[8,64,768]{2,1,0:T(8,128)(2,1)}), bf16[8,64,768]{2,1,0:T(8,128)(2,1)S(1)}, u32[]{:S(2)}, u32[]{:S(2)}) async-start(bf16[8,64,768]{2,1,0:T(8,128)(2,1)} %get-tuple-element.94), calls=%async_computation.1 | async-start | bytes 1572864 | tf_op jit(solution)/shard_map/all_to_all | solution.py:531
  91.7 5.5 %shard_map.260 = (f32[197,768]{1,0:T(8,128)}, bf16[197,384]{1,0:T(8,128)(2,1)}, bf16[197,384]{1,0:T(8,128)(2,1)}, bf16[384,896]{1,0:T(8,128)(2,1)}, bf16[384,896]{1,0:T(8,128)(2,1)}) custom-call(s32[3]{0:T(128)} %pad_add_fusion.ids_ref, bf16[224,768]{1,0:T(8,128)(2,1)} %shard_map.258.pack_ref, bf16[224,768]{1,0:T(8,128)(2,1)} %copy-done.8, ...), custom_call_target="tpu_custom_call" | custom-call | flops 464781312 | bytes 3226836 | tf_op jit(solution)/shard_map/pallas_call | solution.py:508
  97.7 6.4 %shard_map.261 = (bf16[197,768]{1,0:T(8,128)(2,1)}, bf16[384,896]{1,0:T(8,128)(2,1)}, bf16[384,896]{1,0:T(8,128)(2,1)}) custom-call(s32[3]{0:T(128)} %pad_add_fusion.ids_ref, bf16[197,384]{1,0:T(8,128)(2,1)} %get-tuple-element.100.grad_att_ref, bf16[197,384]{1,0:T(8,128)(2,1)} %get-tuple-element.101.grad_v_ref, ...), custom_call_target="tpu_custom_call" | custom-call | flops 697171968 | bytes 2935564 | tf_op jit(solution)/shard_map/pallas_call | solution.py:508
  104.8 4.1 %collective-permute-done.26 = f32[1,2304]{1,0:T(1,128)S(1)} collective-permute-done((f32[1,2304]{1,0:T(1,128)S(1)}, f32[1,2304]{1,0:T(1,128)S(1)}, u32[]{:S(2)}, u32[]{:S(2)}) %collective-permute-start.26) | collective-permute-done | bytes 9248 | tf_op jit(solution)/shard_map/ppermute | solution.py:520
  109.4 0.9 collective-permute-start.17
  110.3 2.1 %add_convert_fusion = bf16[384,896]{1,0:T(8,128)(2,1)} fusion(bf16[384,896]{1,0:T(8,128)(2,1)} %collective-permute-done.22, bf16[384,896]{1,0:T(8,128)(2,1)S(1)} %copy-done.7), kind=kLoop, calls=%fused_computation.2 | loop fusion | flops 1376256 | bytes 2064384 | tf_op jit(solution)/shard_map/convert_element_type | solution.py:732
  112.4 7.1 %all-to-all-start.2 = ((bf16[8,48,896]{2,1,0:T(8,128)(2,1)}), bf16[8,48,896]{2,1,0:T(8,128)(2,1)S(1)}, u32[]{:S(2)}, u32[]{:S(2)}) async-start(bf16[8,48,896]{2,1,0:T(8,128)(2,1)} %bitcast.27), calls=%async_computation.2 | async-start | bytes 1376256 | tf_op jit(solution)/shard_map/all_to_all | solution.py:531
  119.5 2.3 %shard_map.263 = (bf16[4,48,896]{2,1,0:T(8,128)(2,1)}, bf16[4,48,896]{2,1,0:T(8,128)(2,1)}) custom-call(s32[3]{0:T(128)} %pad_add_fusion.ids_ref, bf16[8,48,896]{2,1,0:T(8,128)(2,1)} %bitcast.31, bf16[8,48,896]{2,1,0:T(8,128)(2,1)} %bitcast.12.got_ref), custom_call_target="tpu_custom_call" | custom-call | bytes 1376268 | tf_op jit(solution)/shard_map/pallas_call | solution.py:508
  121.8 2.1 %collective-permute-start.19 = (bf16[4,48,896]{2,1,0:T(8,128)(2,1)}, bf16[4,48,896]{2,1,0:T(8,128)(2,1)S(1)}, u32[]{:S(2)}, u32[]{:S(2)}) collective-permute-start(bf16[4,48,896]{2,1,0:T(8,128)(2,1)} %get-tuple-element.107), channel_id=1, source_target_pairs={{0,2},{2,0},{4,6},{6,4},{8,10},{10,8},{12,14},{14,12},{1,3},{3,1},... | collective-permute-start | bytes 1032200 | tf_op jit(solution)/shard_map/ppermute | solution.py:549
  125.1 2.6 %shard_map.262 = bf16[197,768]{1,0:T(8,128)(2,1)} custom-call(bf16[197,768]{1,0:T(8,128)(2,1)} %get-tuple-element.102.part_ref, bf16[197,768]{1,0:T(8,128)(2,1)} %copy-done.10, bf16[197,768]{1,0:T(8,128)(2,1)} %tok_ref.9, f32[768]{0:T(1024)} %scale_ref.9, f32[768]{0:T(1024)} %shift_ref.9, f32[197,768]{1,0:T(8,128)} %get-tuple-element.103.grad_ref), custom_call_target="tpu_custom_call" | custom-call | bytes 1519104 | tf_op jit(solution)/shard_map/pallas_call | solution.py:508
  127.6 2.3 %shard_map.259 = bf16[197,768]{1,0:T(8,128)(2,1)} custom-call(s32[4,256]{1,0:T(4,128)} %get-tuple-element.84.target_ref, bf16[512,768]{1,0:T(8,128)(2,1)} %bitcast.26), custom_call_target="tpu_custom_call" | custom-call | flops 154927104 | bytes 790528 | tf_op jit(solution)/shard_map/pallas_call | solution.py:508
  129.9 7.2 %collective-permute-done.19.got_ref = bf16[4,48,896]{2,1,0:T(8,128)(2,1)S(1)} collective-permute-done((bf16[4,48,896]{2,1,0:T(8,128)(2,1)}, bf16[4,48,896]{2,1,0:T(8,128)(2,1)S(1)}, u32[]{:S(2)}, u32[]{:S(2)}) %collective-permute-start.19) | collective-permute-done | bytes 344096 | tf_op jit(solution)/shard_map/ppermute | solution.py:549
  137.8 1.9 %shard_map.264 = (bf16[2,48,896]{2,1,0:T(8,128)(2,1)}, bf16[2,48,896]{2,1,0:T(8,128)(2,1)}) custom-call(s32[3]{0:T(128)} %pad_add_fusion.ids_ref, bf16[4,48,896]{2,1,0:T(8,128)(2,1)} %get-tuple-element.106.kept_ref, bf16[4,48,896]{2,1,0:T(8,128)(2,1)} %copy-done.9), custom_call_target="tpu_custom_call" | custom-call | bytes 688140 | tf_op jit(solution)/shard_map/pallas_call | solution.py:508
  139.7 1.5 collective-permute-start.20
  141.2 6.7 %shard_map.268 = f32[768,1536]{1,0:T(8,128)} custom-call(s32[3]{0:T(128)} %pad_add_fusion.ids_ref, bf16[512,768]{1,0:T(8,128)(2,1)} %get-tuple-element.119.a_ref, bf16[512,768]{1,0:T(8,128)(2,1)} %collective-permute-done.24.a2_ref, bf16[512,1536]{1,0:T(8,128)(2,1)} %get-tuple-element.120.b_ref, bf16[512,1536]{1,0:T(8,128)(2,1)} %collective-permute-done.25.b2_ref), custom_call_target="tpu_custom_call" | custom-call | flops 2415919104 | bytes 9000000 | tf_op jit(solution)/shard_map/pallas_call | solution.py:489
  147.9 6.8 %shard_map.269 = f32[1536,768]{1,0:T(8,128)} custom-call(s32[3]{0:T(128)} %pad_add_fusion.ids_ref, bf16[512,1536]{1,0:T(8,128)(2,1)} %get-tuple-element.82.hidden_ref.a_ref, bf16[512,1536]{1,0:T(8,128)(2,1)} %collective-permute-done.27.a2_ref, bf16[512,768]{1,0:T(8,128)(2,1)} %get-tuple-element.123.b_ref, bf16[512,768]{1,0:T(8,128)(2,1)} %collective-permute-done.28.b2_ref), custom_call_target="tpu_custom_call" | custom-call | flops 2415919104 | bytes 9000000 | tf_op jit(solution)/shard_map/pallas_call | solution.py:489
  155.4 1.7 shard_map.265
  157.1 2.4 %collective-permute-start.21 = (bf16[1,48,896]{2,1,0:T(8,128)(2,1)}, bf16[1,48,896]{2,1,0:T(8,128)(2,1)S(1)}, u32[]{:S(2)}, u32[]{:S(2)}) collective-permute-start(bf16[1,48,896]{2,1,0:T(8,128)(2,1)} %get-tuple-element.111), channel_id=1, source_target_pairs={{0,8},{2,10},{4,12},{6,14},{8,0},{10,2},{12,4},{14,6},{1,9},{3,11}... | collective-permute-start | bytes 258056 | tf_op jit(solution)/shard_map/ppermute | solution.py:549
  160.4 0.9 copy-done.3
  161.2 1.8 %shard_map.266 = (f32[48,384]{1,0:T(8,128)}, f32[48,384]{1,0:T(8,128)}, f32[48,128]{1,0:T(8,128)}) custom-call(bf16[8,48,896]{2,1,0:T(8,128)(2,1)} %copy-done.3), custom_call_target="tpu_custom_call" | custom-call | bytes 688128 | tf_op jit(solution)/shard_map/pallas_call | solution.py:508
  164.3 1.7 shard_map.267
  165.9 1.3 collective-permute-start.23
  167.2 1.6 slice_reduce_fusion.2
  168.8 1.4 copy.30
  (100 shorter events, 11.3 us)
Async XLA Ops:
  3.6 35.7 %copy-start.5 = (bf16[1,1536,768]{2,1,0:T(8,128)(2,1)S(1)}, bf16[1,1536,768]{2,1,0:T(8,128)(2,1)}, u32[]{:S(2)}) copy-start(bf16[1,1536,768]{2,1,0:T(8,128)(2,1)} %param.26) | copy-start | bytes 7077892
  3.6 35.7 %all-to-all-start = ((bf16[8,64,768]{2,1,0:T(8,128)(2,1)}), bf16[8,64,768]{2,1,0:T(8,128)(2,1)S(1)}, u32[]{:S(2)}, u32[]{:S(2)}) async-start(bf16[8,64,768]{2,1,0:T(8,128)(2,1)} %bitcast.30), calls=%async_computation | async-start | bytes 1572864 | tf_op jit(solution)/shard_map/all_to_all | solution.py:531
  15.3 8.9 %collective-permute-start = (bf16[197,768]{1,0:T(8,128)(2,1)}, bf16[197,768]{1,0:T(8,128)(2,1)S(1)}, u32[]{:S(2)}, u32[]{:S(2)}) collective-permute-start(bf16[197,768]{1,0:T(8,128)(2,1)} %get-tuple-element.69.part_ref), channel_id=1, source_target_pairs={{0,1},{1,0},{2,3},{3,2},{4,5},{5,4},{6,7},{7,6},{8,9},{9,8},{10,11... | collective-permute-start | bytes 907784 | tf_op jit(solution)/shard_map/ppermute | solution.py:520
  28.1 7.6 %collective-permute-start.1 = (bf16[64,768]{1,0:T(8,128)(2,1)}, bf16[64,768]{1,0:T(8,128)(2,1)S(1)}, u32[]{:S(2)}, u32[]{:S(2)}) collective-permute-start(bf16[64,768]{1,0:T(8,128)(2,1)} %get-tuple-element.74), channel_id=1, source_target_pairs={{0,2},{2,0},{4,6},{6,4},{8,10},{10,8},{12,14},{14,12},{1,3},{3,1},... | collective-permute-start | bytes 294920 | tf_op jit(solution)/shard_map/ppermute | solution.py:526
  29.9 9.1 %collective-permute-start.2 = (bf16[64,768]{1,0:T(8,128)(2,1)}, bf16[64,768]{1,0:T(8,128)(2,1)S(1)}, u32[]{:S(2)}, u32[]{:S(2)}) collective-permute-start(bf16[64,768]{1,0:T(8,128)(2,1)} %get-tuple-element.75), channel_id=1, source_target_pairs={{0,4},{2,6},{4,0},{6,2},{8,12},{10,14},{12,8},{14,10},{1,5},{3,7},... | collective-permute-start | bytes 294920 | tf_op jit(solution)/shard_map/ppermute | solution.py:526
  31.4 11.0 %collective-permute-start.3 = (bf16[64,768]{1,0:T(8,128)(2,1)}, bf16[64,768]{1,0:T(8,128)(2,1)S(1)}, u32[]{:S(2)}, u32[]{:S(2)}) collective-permute-start(bf16[64,768]{1,0:T(8,128)(2,1)} %get-tuple-element.76), channel_id=1, source_target_pairs={{0,6},{2,4},{4,2},{6,0},{8,14},{10,12},{12,10},{14,8},{1,7},{3,5},... | collective-permute-start | bytes 294920 | tf_op jit(solution)/shard_map/ppermute | solution.py:526
  31.6 14.2 %collective-permute-start.4 = (bf16[64,768]{1,0:T(8,128)(2,1)}, bf16[64,768]{1,0:T(8,128)(2,1)S(1)}, u32[]{:S(2)}, u32[]{:S(2)}) collective-permute-start(bf16[64,768]{1,0:T(8,128)(2,1)} %get-tuple-element.77), channel_id=1, source_target_pairs={{0,8},{2,10},{4,12},{6,14},{8,0},{10,2},{12,4},{14,6},{1,9},{3,11}... | collective-permute-start | bytes 294920 | tf_op jit(solution)/shard_map/ppermute | solution.py:526
  34.3 15.2 %collective-permute-start.5 = (bf16[64,768]{1,0:T(8,128)(2,1)}, bf16[64,768]{1,0:T(8,128)(2,1)}, u32[]{:S(2)}, u32[]{:S(2)}) collective-permute-start(bf16[64,768]{1,0:T(8,128)(2,1)} %get-tuple-element.78), channel_id=1, source_target_pairs={{0,10},{2,8},{4,14},{6,12},{8,2},{10,0},{12,6},{14,4},{1,11},{3,9}... | collective-permute-start | bytes 294920 | tf_op jit(solution)/shard_map/ppermute | solution.py:526
  35.7 6.6 %copy-start.20 = (bf16[64,768]{1,0:T(8,128)(2,1)}, bf16[64,768]{1,0:T(8,128)(2,1)S(1)}, u32[]{:S(2)}) copy-start(bf16[64,768]{1,0:T(8,128)(2,1)S(1)} %collective-permute-done.1.refs_1_) | copy-start | bytes 294916
  35.7 13.8 %collective-permute-start.6 = (bf16[64,768]{1,0:T(8,128)(2,1)}, bf16[64,768]{1,0:T(8,128)(2,1)}, u32[]{:S(2)}, u32[]{:S(2)}) collective-permute-start(bf16[64,768]{1,0:T(8,128)(2,1)} %get-tuple-element.79), channel_id=1, source_target_pairs={{0,12},{2,14},{4,8},{6,10},{8,4},{10,6},{12,0},{14,2},{1,13},{3,15... | collective-permute-start | bytes 294920 | tf_op jit(solution)/shard_map/ppermute | solution.py:526
  39.0 3.4 %copy-start.21 = (bf16[64,768]{1,0:T(8,128)(2,1)}, bf16[64,768]{1,0:T(8,128)(2,1)S(1)}, u32[]{:S(2)}) copy-start(bf16[64,768]{1,0:T(8,128)(2,1)S(1)} %collective-permute-done.2.refs_2_) | copy-start | bytes 294916
  39.0 10.5 %collective-permute-start.7 = (bf16[64,768]{1,0:T(8,128)(2,1)}, bf16[64,768]{1,0:T(8,128)(2,1)}, u32[]{:S(2)}, u32[]{:S(2)}) collective-permute-start(bf16[64,768]{1,0:T(8,128)(2,1)} %get-tuple-element.80), channel_id=1, source_target_pairs={{0,14},{2,12},{4,10},{6,8},{8,6},{10,4},{12,2},{14,0},{1,15},{3,13... | collective-permute-start | bytes 294920 | tf_op jit(solution)/shard_map/ppermute | solution.py:526
  39.3 3.1 %copy-start = (bf16[8,64,768]{2,1,0:T(8,128)(2,1)}, bf16[8,64,768]{2,1,0:T(8,128)(2,1)S(1)}, u32[]{:S(2)}) copy-start(bf16[8,64,768]{2,1,0:T(8,128)(2,1)S(1)} %all-to-all-done.cot_ref) | copy-start | bytes 2359300
  42.4 7.1 %copy-start.22 = (bf16[64,768]{1,0:T(8,128)(2,1)}, bf16[64,768]{1,0:T(8,128)(2,1)S(1)}, u32[]{:S(2)}) copy-start(bf16[64,768]{1,0:T(8,128)(2,1)S(1)} %collective-permute-done.3.refs_3_) | copy-start | bytes 294916
  45.8 3.7 %copy-start.23 = (bf16[64,768]{1,0:T(8,128)(2,1)}, bf16[64,768]{1,0:T(8,128)(2,1)S(1)}, u32[]{:S(2)}) copy-start(bf16[64,768]{1,0:T(8,128)(2,1)S(1)} %collective-permute-done.4.refs_4_) | copy-start | bytes 294916
  59.5 7.5 %collective-permute-start.8 = (bf16[64,768]{1,0:T(8,128)(2,1)}, bf16[64,768]{1,0:T(8,128)(2,1)S(1)}, u32[]{:S(2)}, u32[]{:S(2)}) collective-permute-start(bf16[64,768]{1,0:T(8,128)(2,1)} %get-tuple-element.87), channel_id=1, source_target_pairs={{0,2},{2,0},{4,6},{6,4},{8,10},{10,8},{12,14},{14,12},{1,3},{3,1},... | collective-permute-start | bytes 294920 | tf_op jit(solution)/shard_map/ppermute | solution.py:526
  59.6 9.7 %collective-permute-start.9 = (bf16[64,768]{1,0:T(8,128)(2,1)}, bf16[64,768]{1,0:T(8,128)(2,1)S(1)}, u32[]{:S(2)}, u32[]{:S(2)}) collective-permute-start(bf16[64,768]{1,0:T(8,128)(2,1)} %get-tuple-element.88), channel_id=1, source_target_pairs={{0,4},{2,6},{4,0},{6,2},{8,12},{10,14},{12,8},{14,10},{1,5},{3,7},... | collective-permute-start | bytes 294920 | tf_op jit(solution)/shard_map/ppermute | solution.py:526
  63.2 14.9 %collective-permute-start.10 = (bf16[64,768]{1,0:T(8,128)(2,1)}, bf16[64,768]{1,0:T(8,128)(2,1)S(1)}, u32[]{:S(2)}, u32[]{:S(2)}) collective-permute-start(bf16[64,768]{1,0:T(8,128)(2,1)} %get-tuple-element.89), channel_id=1, source_target_pairs={{0,6},{2,4},{4,2},{6,0},{8,14},{10,12},{12,10},{14,8},{1,7},{3,5},... | collective-permute-start | bytes 294920 | tf_op jit(solution)/shard_map/ppermute | solution.py:526
  64.1 14.0 %collective-permute-start.11 = (bf16[64,768]{1,0:T(8,128)(2,1)}, bf16[64,768]{1,0:T(8,128)(2,1)S(1)}, u32[]{:S(2)}, u32[]{:S(2)}) collective-permute-start(bf16[64,768]{1,0:T(8,128)(2,1)} %get-tuple-element.90), channel_id=1, source_target_pairs={{0,8},{2,10},{4,12},{6,14},{8,0},{10,2},{12,4},{14,6},{1,9},{3,11}... | collective-permute-start | bytes 294920 | tf_op jit(solution)/shard_map/ppermute | solution.py:526
  66.9 13.2 %collective-permute-start.12 = (bf16[64,768]{1,0:T(8,128)(2,1)}, bf16[64,768]{1,0:T(8,128)(2,1)S(1)}, u32[]{:S(2)}, u32[]{:S(2)}) collective-permute-start(bf16[64,768]{1,0:T(8,128)(2,1)} %get-tuple-element.91), channel_id=1, source_target_pairs={{0,10},{2,8},{4,14},{6,12},{8,2},{10,0},{12,6},{14,4},{1,11},{3,9}... | collective-permute-start | bytes 294920 | tf_op jit(solution)/shard_map/ppermute | solution.py:526
  67.0 11.0 %copy-start.13 = (bf16[64,768]{1,0:T(8,128)(2,1)}, bf16[64,768]{1,0:T(8,128)(2,1)S(1)}, u32[]{:S(2)}) copy-start(bf16[64,768]{1,0:T(8,128)(2,1)S(1)} %collective-permute-done.8.refs_1_) | copy-start | bytes 294916
  67.0 13.1 %collective-permute-start.13 = (bf16[64,768]{1,0:T(8,128)(2,1)}, bf16[64,768]{1,0:T(8,128)(2,1)S(1)}, u32[]{:S(2)}, u32[]{:S(2)}) collective-permute-start(bf16[64,768]{1,0:T(8,128)(2,1)} %get-tuple-element.92), channel_id=1, source_target_pairs={{0,12},{2,14},{4,8},{6,10},{8,4},{10,6},{12,0},{14,2},{1,13},{3,15... | collective-permute-start | bytes 294920 | tf_op jit(solution)/shard_map/ppermute | solution.py:526
  69.3 8.7 %copy-start.14 = (bf16[64,768]{1,0:T(8,128)(2,1)}, bf16[64,768]{1,0:T(8,128)(2,1)S(1)}, u32[]{:S(2)}) copy-start(bf16[64,768]{1,0:T(8,128)(2,1)S(1)} %collective-permute-done.9.refs_2_) | copy-start | bytes 294916
  69.3 10.8 %collective-permute-start.14 = (bf16[64,768]{1,0:T(8,128)(2,1)}, bf16[64,768]{1,0:T(8,128)(2,1)S(1)}, u32[]{:S(2)}, u32[]{:S(2)}) collective-permute-start(bf16[64,768]{1,0:T(8,128)(2,1)} %get-tuple-element.93), channel_id=1, source_target_pairs={{0,14},{2,12},{4,10},{6,8},{8,6},{10,4},{12,2},{14,0},{1,15},{3,13... | collective-permute-start | bytes 294920 | tf_op jit(solution)/shard_map/ppermute | solution.py:526
  83.2 7.7 %collective-permute-start.16 = (bf16[224,768]{1,0:T(8,128)(2,1)}, bf16[224,768]{1,0:T(8,128)(2,1)S(1)}, u32[]{:S(2)}, u32[]{:S(2)}) collective-permute-start(bf16[224,768]{1,0:T(8,128)(2,1)} %shard_map.258.pack_ref), channel_id=1, source_target_pairs={{0,1},{1,0},{2,3},{3,2},{4,5},{5,4},{6,7},{7,6},{8,9},{9,8},{10,11... | collective-permute-start | bytes 1032200 | tf_op jit(solution)/shard_map/ppermute | solution.py:520
  84.7 27.7 %all-to-all-start.1 = ((bf16[8,64,768]{2,1,0:T(8,128)(2,1)}), bf16[8,64,768]{2,1,0:T(8,128)(2,1)S(1)}, u32[]{:S(2)}, u32[]{:S(2)}) async-start(bf16[8,64,768]{2,1,0:T(8,128)(2,1)} %get-tuple-element.94), calls=%async_computation.1 | async-start | bytes 1572864 | tf_op jit(solution)/shard_map/all_to_all | solution.py:531
  90.9 50.3 %collective-permute-start.25 = (bf16[512,1536]{1,0:T(8,128)(2,1)}, bf16[512,1536]{1,0:T(8,128)(2,1)}, u32[]{:S(2)}, u32[]{:S(2)}) collective-permute-start(bf16[512,1536]{1,0:T(8,128)(2,1)} %get-tuple-element.120.b_ref), channel_id=1, source_target_pairs={{0,16},{16,0},{1,17},{17,1},{2,18},{18,2},{3,19},{19,3},{4,20},{20... | collective-permute-start | bytes 4718600 | tf_op jit(solution)/shard_map/ppermute | solution.py:520
  91.6 12.6 %copy-start.1 = (bf16[512,1536]{1,0:T(8,128)(2,1)S(1)}, bf16[512,1536]{1,0:T(8,128)(2,1)}, u32[]{:S(2)}) copy-start(bf16[512,1536]{1,0:T(8,128)(2,1)} %get-tuple-element.82.hidden_ref.a_ref) | copy-start | bytes 4718596
  91.7 13.0 %copy-start.25 = (f32[1,1536]{1,0:T(1,128)S(1)}, f32[1,1536]{1,0:T(1,128)}, u32[]{:S(2)}) copy-start(f32[1,1536]{1,0:T(1,128)} %get-tuple-element.121) | copy-start | bytes 18436
  91.7 13.0 %copy-start.26 = (f32[1,768]{1,0:T(1,128)S(1)}, f32[1,768]{1,0:T(1,128)}, u32[]{:S(2)}) copy-start(f32[1,768]{1,0:T(1,128)} %get-tuple-element.122) | copy-start | bytes 9220
  97.2 13.1 %copy-start.7 = (bf16[384,896]{1,0:T(8,128)(2,1)S(1)}, bf16[384,896]{1,0:T(8,128)(2,1)}, u32[]{:S(2)}) copy-start(bf16[384,896]{1,0:T(8,128)(2,1)} %get-tuple-element.112) | copy-start | bytes 2064388
  97.2 11.9 %collective-permute-start.22 = (bf16[384,896]{1,0:T(8,128)(2,1)}, bf16[384,896]{1,0:T(8,128)(2,1)}, u32[]{:S(2)}, u32[]{:S(2)}) collective-permute-start(bf16[384,896]{1,0:T(8,128)(2,1)} %get-tuple-element.113), channel_id=1, source_target_pairs={{0,16},{16,0},{1,17},{17,1},{2,18},{18,2},{3,19},{19,3},{4,20},{20... | collective-permute-start | bytes 2064392 | tf_op jit(solution)/shard_map/ppermute | solution.py:520
  104.2 5.3 %collective-permute-start.18 = (bf16[384,896]{1,0:T(8,128)(2,1)}, bf16[384,896]{1,0:T(8,128)(2,1)}, u32[]{:S(2)}, u32[]{:S(2)}) collective-permute-start(bf16[384,896]{1,0:T(8,128)(2,1)} %get-tuple-element.105), channel_id=1, source_target_pairs={{0,16},{16,0},{1,17},{17,1},{2,18},{18,2},{3,19},{19,3},{4,20},{20... | collective-permute-start | bytes 2064392 | tf_op jit(solution)/shard_map/ppermute | solution.py:520
  104.2 43.7 %collective-permute-start.27 = (bf16[512,1536]{1,0:T(8,128)(2,1)S(1)}, bf16[512,1536]{1,0:T(8,128)(2,1)}, u32[]{:S(2)}, u32[]{:S(2)}) collective-permute-start(bf16[512,1536]{1,0:T(8,128)(2,1)S(1)} %copy-done.1), channel_id=1, source_target_pairs={{0,16},{16,0},{1,17},{17,1},{2,18},{18,2},{3,19},{19,3},{4,20},{20... | collective-permute-start | bytes 4718600 | tf_op jit(solution)/shard_map/ppermute | solution.py:520
  104.7 4.2 %collective-permute-start.26 = (f32[1,2304]{1,0:T(1,128)S(1)}, f32[1,2304]{1,0:T(1,128)S(1)}, u32[]{:S(2)}, u32[]{:S(2)}) collective-permute-start(f32[1,2304]{1,0:T(1,128)S(1)} %constant_dynamic-update-slice_fusion), channel_id=1, source_target_pairs={{0,16},{16,0},{1,17},{17,1},{2,18},{18,2},{3,19},{19,3},{4,20},{20... | collective-permute-start | bytes 27656 | tf_op jit(solution)/shard_map/ppermute | solution.py:520
  108.9 30.8 %collective-permute-start.24 = (bf16[512,768]{1,0:T(8,128)(2,1)}, bf16[512,768]{1,0:T(8,128)(2,1)}, u32[]{:S(2)}, u32[]{:S(2)}) collective-permute-start(bf16[512,768]{1,0:T(8,128)(2,1)} %get-tuple-element.119.a_ref), channel_id=1, source_target_pairs={{0,16},{16,0},{1,17},{17,1},{2,18},{18,2},{3,19},{19,3},{4,20},{20... | collective-permute-start | bytes 2359304 | tf_op jit(solution)/shard_map/ppermute | solution.py:520
  109.0 38.9 %collective-permute-start.28 = (bf16[512,768]{1,0:T(8,128)(2,1)}, bf16[512,768]{1,0:T(8,128)(2,1)}, u32[]{:S(2)}, u32[]{:S(2)}) collective-permute-start(bf16[512,768]{1,0:T(8,128)(2,1)} %get-tuple-element.123.b_ref), channel_id=1, source_target_pairs={{0,16},{16,0},{1,17},{17,1},{2,18},{18,2},{3,19},{19,3},{4,20},{20... | collective-permute-start | bytes 2359304 | tf_op jit(solution)/shard_map/ppermute | solution.py:520
  109.4 12.4 %collective-permute-start.17 = (bf16[197,768]{1,0:T(8,128)(2,1)}, bf16[197,768]{1,0:T(8,128)(2,1)S(1)}, u32[]{:S(2)}, u32[]{:S(2)}) collective-permute-start(bf16[197,768]{1,0:T(8,128)(2,1)} %get-tuple-element.102.part_ref), channel_id=1, source_target_pairs={{0,1},{1,0},{2,3},{3,2},{4,5},{5,4},{6,7},{7,6},{8,9},{9,8},{10,11... | collective-permute-start | bytes 907784 | tf_op jit(solution)/shard_map/ppermute | solution.py:520
  112.4 15.2 %copy-start.2 = (bf16[8,64,768]{2,1,0:T(8,128)(2,1)}, bf16[8,64,768]{2,1,0:T(8,128)(2,1)S(1)}, u32[]{:S(2)}) copy-start(bf16[8,64,768]{2,1,0:T(8,128)(2,1)S(1)} %all-to-all-done.1) | copy-start | bytes 2359300
  112.4 47.9 %all-to-all-start.2 = ((bf16[8,48,896]{2,1,0:T(8,128)(2,1)}), bf16[8,48,896]{2,1,0:T(8,128)(2,1)S(1)}, u32[]{:S(2)}, u32[]{:S(2)}) async-start(bf16[8,48,896]{2,1,0:T(8,128)(2,1)} %bitcast.27), calls=%async_computation.2 | async-start | bytes 1376256 | tf_op jit(solution)/shard_map/all_to_all | solution.py:531
  121.8 3.2 %copy-start.10 = (bf16[197,768]{1,0:T(8,128)(2,1)}, bf16[197,768]{1,0:T(8,128)(2,1)S(1)}, u32[]{:S(2)}) copy-start(bf16[197,768]{1,0:T(8,128)(2,1)S(1)} %collective-permute-done.17.part2_ref) | copy-start | bytes 907780
  121.8 15.3 %collective-permute-start.19 = (bf16[4,48,896]{2,1,0:T(8,128)(2,1)}, bf16[4,48,896]{2,1,0:T(8,128)(2,1)S(1)}, u32[]{:S(2)}, u32[]{:S(2)}) collective-permute-start(bf16[4,48,896]{2,1,0:T(8,128)(2,1)} %get-tuple-element.107), channel_id=1, source_target_pairs={{0,2},{2,0},{4,6},{6,4},{8,10},{10,8},{12,14},{14,12},{1,3},{3,1},... | collective-permute-start | bytes 1032200 | tf_op jit(solution)/shard_map/ppermute | solution.py:549
  137.1 22.4 %collective-permute-start.15 = (bf16[197,768]{1,0:T(8,128)(2,1)}, bf16[197,768]{1,0:T(8,128)(2,1)S(1)}, u32[]{:S(2)}, u32[]{:S(2)}) collective-permute-start(bf16[197,768]{1,0:T(8,128)(2,1)} %shard_map.259), channel_id=1, source_target_pairs={{0,1},{1,0},{2,3},{3,2},{4,5},{5,4},{6,7},{7,6},{8,9},{9,8},{10,11... | collective-permute-start | bytes 907784 | tf_op jit(solution)/shard_map/ppermute | solution.py:520
  139.7 15.0 %collective-permute-start.20 = (bf16[2,48,896]{2,1,0:T(8,128)(2,1)}, bf16[2,48,896]{2,1,0:T(8,128)(2,1)S(1)}, u32[]{:S(2)}, u32[]{:S(2)}) collective-permute-start(bf16[2,48,896]{2,1,0:T(8,128)(2,1)} %get-tuple-element.109), channel_id=1, source_target_pairs={{0,4},{2,6},{4,0},{6,2},{8,12},{10,14},{12,8},{14,10},{1,5},{3,7},... | collective-permute-start | bytes 516104 | tf_op jit(solution)/shard_map/ppermute | solution.py:549
  147.9 11.6 %copy-start.4 = (f32[197,768]{1,0:T(8,128)S(1)}, f32[197,768]{1,0:T(8,128)}, u32[]{:S(2)}) copy-start(f32[197,768]{1,0:T(8,128)} %get-tuple-element.71.mixed_ref) | copy-start | bytes 1815556
  147.9 11.6 %copy-start.6 = (bf16[197,768]{1,0:T(8,128)(2,1)S(1)}, bf16[197,768]{1,0:T(8,128)(2,1)}, u32[]{:S(2)}) copy-start(bf16[197,768]{1,0:T(8,128)(2,1)} %shard_map.259) | copy-start | bytes 907780
  157.1 6.5 %collective-permute-start.21 = (bf16[1,48,896]{2,1,0:T(8,128)(2,1)}, bf16[1,48,896]{2,1,0:T(8,128)(2,1)S(1)}, u32[]{:S(2)}, u32[]{:S(2)}) collective-permute-start(bf16[1,48,896]{2,1,0:T(8,128)(2,1)} %get-tuple-element.111), channel_id=1, source_target_pairs={{0,8},{2,10},{4,12},{6,14},{8,0},{10,2},{12,4},{14,6},{1,9},{3,11}... | collective-permute-start | bytes 258056 | tf_op jit(solution)/shard_map/ppermute | solution.py:549
  165.9 4.3 %collective-permute-start.23 = (f32[48,128]{1,0:T(8,128)}, f32[48,128]{1,0:T(8,128)S(1)}, u32[]{:S(2)}, u32[]{:S(2)}) collective-permute-start(f32[48,128]{1,0:T(8,128)} %get-tuple-element.115), channel_id=1, source_target_pairs={{0,1},{1,0},{2,3},{3,2},{4,5},{5,4},{6,7},{7,6},{8,9},{9,8},{10,11... | collective-permute-start | bytes 73736 | tf_op jit(solution)/shard_map/ppermute | solution.py:520
  (11 other events, 10.5 us)
where the time goes:
time: 173 us; the launch traced here: 172 us
  Pallas kernels  68.2 us (39%)
  starting transfers between devices  57.4 us (33%)
  waiting for transfers between devices  28.4 us (16%)
  local copies, waits for them, and re-layouts  9.46 us (5%)
  other arithmetic  4.29 us (2%)
  matrix products  3.08 us (2%)
    pallas_call x13, Pallas kernels, call(): pl.pallas_call(kernel, out_shape=tuple((jax.ShapeDtypeStruct(s, d) for s,...  38.4 us
    ppermute x14, starting transfers between devices, xor_exchange(): lax.ppermute(blocks[k], 'expert', [(i, i ^ k) for i in range(count)])  23.3 us
    all_to_all x3, starting transfers between devices, all_to_all(): return lax.all_to_all(x, 'expert', split_axis=0, concat_axis=0, tiled=True)  20.7 us
    pallas_call x2, Pallas kernels, weight_grad(): pl.pallas_call(weight_grad_kernel, grid=(rows // tile,), out_shape=jax.Sh...  13.5 us
    ppermute x12, waiting for transfers between devices, swap(): return lax.ppermute(x, axis, [(0, 1), (1, 0)])  11.5 us
    pallas_call x1, Pallas kernels, expert(): pl.pallas_call(functools.partial(expert_kernel, (near, capacity, cap_pad,...  9.98 us
    ppermute x14, waiting for transfers between devices, xor_exchange(): lax.ppermute(blocks[k], 'expert', [(i, i ^ k) for i in range(count)])  9.13 us
    ppermute x3, waiting for transfers between devices, reduce_dense(): lax.ppermute(send, 'expert', [(i, i ^ 1 << bit) for i in range(count)])  7.76 us
  transfers between devices with their start and end apart: 32, of which 7 were waited for; matrix products, arithmetic and copies ran while one was open for 6% of the time, Pallas kernels for 30%

commit v1 on v0

--- a/solution.py
+++ b/solution.py
@@ -14,6 +14,7 @@
 F32 = jnp.float32
 I32 = jnp.int32
 LANES = 128
+DP, EX, TE = "dp", "expert", "tensor"
 SCALING = HEAD_DIM ** (-0.5)
 
 PARAMS = pltpu.CompilerParams(vmem_limit_bytes=60 * 1024 * 1024)
@@ -180,86 +181,65 @@
     in0 = ids == target_ref[2:3, 0:rows]
     in1 = ids == target_ref[3:4, 0:rows]
     gates = jnp.sum(jnp.where(in0, gate0, jnp.where(in1, gate1, 0.0)), axis=1, keepdims=True)
-    place = jnp.where(in0 | in1, 1.0, 0.0).astype(BF)
+    picked = dot32(jnp.where(in0 | in1, 1.0, 0.0).astype(BF), normed)
     for k in range(experts):
         span = slice(k * cap_pad, (k + 1) * cap_pad)
-        block = dot32(place[span], normed)
+        block = picked[span]
         block_refs[k][:, LANES:] = block[:, LANES:].astype(BF)
         block_refs[k][:, :LANES] = with_pad_row(block[:, :LANES], gates[span], capacity).astype(BF)
 
 
 def expert_kernel(sizes, ids_ref, raw_ref, cot_ref, bias2_ref, w_ref, b_ref, *refs):
-    blocks, capacity, cap_pad, held, base = sizes
+    blocks, capacity, cap_pad = sizes
     row_refs = refs[:blocks]
-    x_ref, gate_ref, hidden_ref, pre_ref, bsum_ref = refs[blocks + held : blocks + held + 5]
-    back_refs = refs[blocks + held + 5 : 2 * blocks + held + 5]
-    acc_ref, sg_ref = refs[2 * blocks + held + 5 :]
+    x_ref, gate_ref, hidden_ref, pre_ref, sent_ref = refs[blocks : blocks + 5]
+    back_refs = refs[blocks + 5 : 2 * blocks + 5]
+    acc_ref, sg_ref = refs[2 * blocks + 5 :]
     step, last = pl.program_id(0), pl.num_programs(0) - 1
+
+    def place(k):
+        return pl.ds(pl.multiple_of((k ^ ids_ref[0]) * cap_pad, cap_pad), cap_pad)
 
     @pl.when(step == 0)
     def _():
-        acc_ref[...] = jnp.zeros_like(acc_ref)
         first = jnp.where(ids_ref[1] == 0, 1.0, 0.0)
         for k in range(blocks):
-            span = slice(k * cap_pad, (k + 1) * cap_pad)
+            span = place(k)
             x_ref[span, :] = row_refs[k][...]
             gate = from_pad_row(row_refs[k][:, :LANES].astype(F32), capacity)
             gate_ref[span, :] = jnp.broadcast_to(gate, (cap_pad, LANES))
-            cot = cot_ref[(base + k) ^ ids_ref[0]].astype(F32)
+            cot = cot_ref[span, :].astype(F32)
             side = jnp.sum(cot * bias2_ref[...], axis=1, keepdims=True)
             sg_ref[span, :] = jnp.broadcast_to(first * side, (cap_pad, LANES))
+            sent_ref[span, :] = (gate * cot).astype(BF)
 
     w = w_ref[...]
     pre_act = dot32(x_ref[...], w) + b_ref[...]
-    total = jnp.zeros(b_ref.shape, F32)
     for k in range(blocks):
         span = slice(k * cap_pad, (k + 1) * cap_pad)
         value, slope = gelu_both(pre_act[span])
-        raw = raw_ref[(base + k) ^ ids_ref[0]]
+        raw = raw_ref[span, :]
         hidden_ref[span, :] = value.astype(BF)
-        grad = gate_ref[span, 0:1] * raw * slope
-        pre_ref[span, :] = grad.astype(BF)
-        total = total + jnp.sum(grad, axis=0, keepdims=True)
+        pre_ref[span, :] = (gate_ref[span, 0:1] * raw * slope).astype(BF)
         side = jnp.sum(value * raw, axis=1, keepdims=True)
         sg_ref[span, :] = sg_ref[span, :] + jnp.broadcast_to(side, (cap_pad, LANES))
-    bsum_ref[...] = total
-    acc_ref[...] += dot_nt(pre_ref[...], w)
+    grad = dot_nt(pre_ref[...], w)
+
+    @pl.when(step == 0)
+    def _():
+        acc_ref[...] = grad
+
+    @pl.when(step > 0)
+    def _():
+        acc_ref[...] += grad
 
     @pl.when(step == last)
     def _():
         for k in range(blocks):
-            span = slice(k * cap_pad, (k + 1) * cap_pad)
+            span = place(k)
             back_refs[k][:, LANES:] = acc_ref[span, LANES:].astype(BF)
             first = with_pad_row(acc_ref[span, :LANES], sg_ref[span, 0:1], capacity)
             back_refs[k][:, :LANES] = first.astype(BF)
-
-
-def expert_out_kernel(
-    sizes, ids_ref, gate_ref, cot_ref, bias2_ref, hidden_ref, w_ref, out_ref, sent_ref, bsum_ref, acc_ref
-):
-    experts, _, cap_pad = sizes
-    step, last = pl.program_id(0), pl.num_programs(0) - 1
-
-    @pl.when(step == 0)
-    def _():
-        acc_ref[...] = jnp.zeros_like(acc_ref)
-        total = jnp.zeros(bsum_ref.shape, F32)
-        for k in range(experts):
-            span = slice(k * cap_pad, (k + 1) * cap_pad)
-            sent = gate_ref[span, 0:1] * cot_ref[k ^ ids_ref[0]].astype(F32)
-            total = total + jnp.sum(sent, axis=0, keepdims=True)
-            sent_ref[span, :] = sent.astype(BF)
-        bsum_ref[...] = total
-
-    acc_ref[...] += dot32(hidden_ref[...], w_ref[...])
-
-    @pl.when(step == last)
-    def _():
-        bias = jnp.where(ids_ref[1] == 0, 1.0, 0.0) * bias2_ref[...]
-        for k in range(experts):
-            span = slice(k * cap_pad, (k + 1) * cap_pad)
-            value = gate_ref[span, 0:1] * (acc_ref[span, :] + bias)
-            out_ref[k ^ ids_ref[0]] = value.astype(BF)
 
 
 def combine_kernel(sizes, target_ref, *refs):
@@ -443,34 +423,40 @@
     out_ref[...] = (grad_ref[...] + norm_back(grad, x_hat, inv_std, row(scale_ref))).astype(BF)
 
 
-def hop_kernel(bit, ids_ref, kept_ref, got_ref, keep_ref, send_ref):
-    mine = (ids_ref[0] >> bit) & 1
-    for j in range(keep_ref.shape[0]):
-        a, b = 2 * j + mine, 2 * j + 1 - mine
-        keep_ref[j] = (kept_ref[a].astype(F32) + got_ref[a].astype(F32)).astype(BF)
-        send_ref[j] = (kept_ref[b].astype(F32) + got_ref[b].astype(F32)).astype(BF)
-
-
-def early_end_kernel(part_ref, w_out_ref, v_ref, small_ref):
-    hidden = v_ref.shape[1]
+def early_end_kernel(part_ref, w_out_ref, v_ref, router_ref, b_ref, scale_ref, shift_ref, turn_ref):
+    piece, hidden = v_ref.shape
+    experts = router_ref.shape[0]
     total = part_ref[0].astype(F32)
     for k in range(1, part_ref.shape[0]):
         total = total + part_ref[k].astype(F32)
     w_out_ref[...] = total[:, :hidden]
     v_ref[...] = total[:, hidden : 2 * hidden]
-    small_ref[...] = total[:, 2 * hidden :]
-
-
-def late_end_kernel(kept_ref, got_ref, v_ref, qkv_ref, ln1_ref):
-    hidden = v_ref.shape[1]
+    turn_ref[...] = jnp.zeros_like(turn_ref)
+    turn_ref[0:piece, :] = total[:, 2 * hidden :]
+    turned = turn_ref[...].T
+    router_ref[...] = turned[0:experts, 0:piece]
+    b_ref[...] = turned[experts : experts + 1, 0:piece]
+    scale_ref[...] = turned[experts + 1 : experts + 2, 0:piece]
+    shift_ref[...] = turned[experts + 2 : experts + 3, 0:piece]
+
+
+def late_end_kernel(kept_ref, got_ref, v_ref, qkv_ref, ln1_ref, turn_ref):
+    piece, hidden = v_ref.shape
     total = kept_ref[0].astype(F32) + got_ref[0].astype(F32)
+    turn_ref[...] = jnp.zeros_like(turn_ref)
+    turn_ref[0:piece, :] = total[:, 2 * hidden :]
+    ln1_ref[...] = turn_ref[...].T[0:8]
     qkv_ref[0] = total[:, :hidden]
     qkv_ref[1] = total[:, hidden : 2 * hidden]
     qkv_ref[2] = v_ref[...]
-    ln1_ref[...] = total[:, 2 * hidden :]
-
-
-def weight_grad_kernel(ids_ref, a_ref, a2_ref, b_ref, b2_ref, out_ref):
+
+
+def weight_grad_kernel(ids_ref, a_ref, a2_ref, b_ref, b2_ref, out_ref, sum_ref):
+    @pl.when(pl.program_id(0) == 0)
+    def _():
+        own = jnp.sum(b_ref[...].astype(F32), axis=0, keepdims=True)
+        sum_ref[...] = own + jnp.sum(b2_ref[...].astype(F32), axis=0, keepdims=True)
+
     @pl.when(ids_ref[2] == 0)
     def _():
         out_ref[...] = dot_tn(a_ref[...], b_ref[...]) + dot_tn(a2_ref[...], b2_ref[...])
@@ -489,9 +475,15 @@
     return pl.pallas_call(
         weight_grad_kernel,
         grid=(rows // tile,),
-        out_shape=jax.ShapeDtypeStruct((rows, cols), F32),
+        out_shape=[
+            jax.ShapeDtypeStruct((rows, cols), F32),
+            jax.ShapeDtypeStruct((1, cols), F32),
+        ],
         in_specs=[pl.BlockSpec(memory_space=pltpu.SMEM), left, left, right, right],
-        out_specs=pl.BlockSpec((tile, cols), lambda i: (i, 0)),
+        out_specs=[
+            pl.BlockSpec((tile, cols), lambda i: (i, 0)),
+            pl.BlockSpec((1, cols), lambda i: (0, 0)),
+        ],
         compiler_params=PARAMS,
         cost_estimate=pl.CostEstimate(
             flops=4 * slots * rows * cols, bytes_accessed=9_000_000, transcendentals=0
@@ -523,30 +515,34 @@
 def xor_exchange(blocks, count, order):
     outs = {}
     for k in order:
-        outs[k] = lax.ppermute(blocks[k], "expert", [(i, i ^ k) for i in range(count)])
+        outs[k] = lax.ppermute(blocks[k], EX, [(i, i ^ k) for i in range(count)])
     return outs
 
 
 def all_to_all(x):
-    return lax.all_to_all(x, "expert", split_axis=0, concat_axis=0, tiled=True)
+    return lax.all_to_all(x, EX, split_axis=0, concat_axis=0, tiled=True)
 
 
 def reduce_dense(ids, keep, send):
-    count = lax.axis_size("expert")
+    count = lax.axis_size(EX)
     piece = keep.shape[0] // count
     cols = keep.shape[1]
-    got = swap(send, "dp").reshape(count, piece, cols)
+    got = swap(send, DP).reshape(count, piece, cols)
     keep = keep.reshape(count, piece, cols)
     bit, left = 0, count
     while left > 1:
         left //= 2
-        keep, send = call(
-            functools.partial(hop_kernel, bit),
-            [((left, piece, cols), BF), ((left, piece, cols), BF)],
-            ids, keep, got,
-            scalars=1,
-        )
-        got = lax.ppermute(send, "expert", [(i, i ^ (1 << bit)) for i in range(count)])
+        mine = (ids[0] >> bit) & 1
+        pair = (left, 2, piece, cols)
+
+        def half_sum(which):
+            return (
+                lax.dynamic_index_in_dim(keep.reshape(pair), which, 1, keepdims=False).astype(F32)
+                + lax.dynamic_index_in_dim(got.reshape(pair), which, 1, keepdims=False).astype(F32)
+            ).astype(BF)
+
+        send, keep = half_sum(1 - mine), half_sum(mine)
+        got = lax.ppermute(send, EX, [(i, i ^ (1 << bit)) for i in range(count)])
         bit += 1
     return keep, got
 
@@ -570,9 +566,9 @@
 ):
     rows, width = tokens.shape
     experts = w_router.shape[1]
-    count = lax.axis_size("expert")
+    count = lax.axis_size(EX)
     ids = jnp.stack(
-        [lax.axis_index("expert"), lax.axis_index("tensor"), lax.axis_index("dp")]
+        [lax.axis_index(EX), lax.axis_index(TE), lax.axis_index(DP)]
     ).astype(I32)
     capacity = (5 * rows + 2 * experts - 1) // (2 * experts)
     cap_pad = round_up(capacity + 1, 16)
@@ -600,109 +596,65 @@
         tokens, ln1_scale, ln1_bias, w3, w_out,
         flops=8 * rows * width * hidden,
     )
-    part_other = swap(part, "tensor")
+    part_other = swap(part, TE)
     mixed, probs, *blocks = call(
         functools.partial(middle_kernel, sizes),
         [((rows, width), F32), ((experts, rows), F32)] + [((cap_pad, width), BF)] * experts,
         tokens, part, part_other, b_out, ln2_scale, ln2_bias, router_t, routes_t, target,
         flops=2 * slots * rows * width,
     )
-    near = experts
     order = tuple(range(experts - 1, 0, -1))
     received = xor_exchange(blocks, count, order)
     received[0] = blocks[0]
 
-    tile = 384
-    grid = inner // tile
+    tile = 512
     whole = lambda shape: pl.BlockSpec(shape, lambda f: (0,) * len(shape))
-    smem = pl.BlockSpec(memory_space=pltpu.SMEM)
-    anywhere = pl.BlockSpec(memory_space=pl.ANY)
-    raw = dot_nt(cot_rows.reshape(slots, width), w_exp_out).reshape(experts, cap_pad, inner)
-
-    def expert(which, held):
-        span = near * cap_pad
-        at = lambda f: (which, f)
-        fixed = lambda f: (which, 0)
-        shapes = [
+    wide = pl.BlockSpec((slots, tile), lambda f: (0, f))
+    cot_rows = cot_rows.reshape(slots, width)
+    raw = dot_nt(cot_rows, w_exp_out)
+    outs = pl.pallas_call(
+        functools.partial(expert_kernel, (experts, capacity, cap_pad)),
+        grid=(inner // tile,),
+        out_shape=[
             jax.ShapeDtypeStruct((slots, width), BF),
             jax.ShapeDtypeStruct((slots, LANES), F32),
             jax.ShapeDtypeStruct((slots, inner), BF),
             jax.ShapeDtypeStruct((slots, inner), BF),
+            jax.ShapeDtypeStruct((slots, width), BF),
         ]
-        return pl.pallas_call(
-            functools.partial(expert_kernel, (near, capacity, cap_pad, len(held), which * near)),
-            grid=(grid,),
-            out_shape=shapes
-            + [jax.ShapeDtypeStruct((1, inner), F32)]
-            + [jax.ShapeDtypeStruct((cap_pad, width), BF)] * near,
-            in_specs=[
-                smem,
-                pl.BlockSpec((experts, cap_pad, tile), lambda f: (0, 0, f)),
-                whole((experts, cap_pad, width)),
-                whole((1, width)),
-                pl.BlockSpec((width, tile), lambda f: (0, f)),
-                pl.BlockSpec((1, tile), lambda f: (0, f)),
-            ]
-            + [whole((cap_pad, width))] * near
-            + [anywhere] * len(held),
-            out_specs=[
-                pl.BlockSpec((span, width), fixed),
-                pl.BlockSpec((span, LANES), fixed),
-                pl.BlockSpec((span, tile), at),
-                pl.BlockSpec((span, tile), at),
-                pl.BlockSpec((1, tile), lambda f: (0, f)),
-            ]
-            + [whole((cap_pad, width))] * near,
-            input_output_aliases={6 + near + i: i for i in range(len(held))},
-            scratch_shapes=[pltpu.VMEM((span, width), F32), pltpu.VMEM((span, LANES), F32)],
-            compiler_params=PARAMS,
-            cost_estimate=pl.CostEstimate(
-                flops=2 * slots * width * inner, bytes_accessed=6_000_000, transcendentals=0
-            ),
-        )(
-            ids, raw, cot_rows, b_exp_out, w_in, b_in,
-            *[received[which * near + i] for i in range(near)],
-            *held,
-        )
-
-    outs = expert(0, ())
-    x_rows, gate, hidden_act, grad_pre, grad_b1 = outs[:5]
+        + [jax.ShapeDtypeStruct((cap_pad, width), BF)] * experts,
+        in_specs=[
+            pl.BlockSpec(memory_space=pltpu.SMEM),
+            wide,
+            whole((slots, width)),
+            whole((1, width)),
+            pl.BlockSpec((width, tile), lambda f: (0, f)),
+            pl.BlockSpec((1, tile), lambda f: (0, f)),
+        ]
+        + [whole((cap_pad, width))] * experts,
+        out_specs=[whole((slots, width)), whole((slots, LANES)), wide, wide, whole((slots, width))]
+        + [whole((cap_pad, width))] * experts,
+        scratch_shapes=[pltpu.VMEM((slots, width), F32), pltpu.VMEM((slots, LANES), F32)],
+        compiler_params=PARAMS,
+        cost_estimate=pl.CostEstimate(
+            flops=4 * slots * width * inner, bytes_accessed=12_000_000, transcendentals=0
+        ),
+    )(ids, raw, cot_rows, b_exp_out, w_in, b_in, *[received[k] for k in range(experts)])
+    x_rows, gate, hidden_act, grad_pre, grad_sent = outs[:5]
     back = xor_exchange(outs[5:], count, order)
     back[0] = outs[5]
-    out_rows, grad_sent, grad_b2 = pl.pallas_call(
-        functools.partial(expert_out_kernel, (experts, capacity, cap_pad)),
-        grid=(grid,),
-        out_shape=[
-            jax.ShapeDtypeStruct((experts, cap_pad, width), BF),
-            jax.ShapeDtypeStruct((slots, width), BF),
-            jax.ShapeDtypeStruct((1, width), F32),
-        ],
-        in_specs=[
-            smem,
-            whole((slots, LANES)),
-            whole((experts, cap_pad, width)),
-            whole((1, width)),
-            pl.BlockSpec((slots, tile), lambda f: (0, f)),
-            pl.BlockSpec((tile, width), lambda f: (f, 0)),
-        ],
-        out_specs=[whole((experts, cap_pad, width)), whole((slots, width)), whole((1, width))],
-        scratch_shapes=[pltpu.VMEM((slots, width), F32)],
-        compiler_params=PARAMS,
-        cost_estimate=pl.CostEstimate(
-            flops=2 * slots * width * inner, bytes_accessed=6_000_000, transcendentals=0
-        ),
-        name="expert_out",
-    )(ids, gate, cot_rows, b_exp_out, hidden_act, w_exp_out)
-    x_other = swap(x_rows, "dp")
-    pre_other = swap(grad_pre, "dp")
-    hidden_other = swap(hidden_act, "dp")
-    sent_other = swap(grad_sent, "dp")
-    grad_w_in = weight_grad(ids, x_rows, x_other, grad_pre, pre_other)
-    grad_w_exp_out = weight_grad(ids, hidden_act, hidden_other, grad_sent, sent_other)
-    biases = jnp.concatenate([grad_b1, grad_b2], axis=1)
-    biases = biases + swap(biases, "dp")
+    own_bias = jnp.where(lax.axis_index(TE) == 0, b_exp_out, 0.0)
+    out_rows = gate[:, :1] * (dot32(hidden_act, w_exp_out) + own_bias)
+    out_rows = out_rows.astype(BF).reshape(experts, cap_pad, width)
+    x_other = swap(x_rows, DP)
+    pre_other = swap(grad_pre, DP)
+    hidden_other = swap(hidden_act, DP)
+    sent_other = swap(grad_sent, DP)
+    grad_w_in, grad_b_in = weight_grad(ids, x_rows, x_other, grad_pre, pre_other)
+    grad_w_exp_out, grad_b_exp_out = weight_grad(
+        ids, hidden_act, hidden_other, grad_sent, sent_other
+    )
     body = round_up(rows, 16)
-    target, out_rows = lax.optimization_barrier((target, out_rows))
     (pack,) = call(
         functools.partial(combine_kernel, sizes),
         [((body + 16, width), BF)],
@@ -710,7 +662,7 @@
         scratch=[pltpu.VMEM((slots, width), BF)],
         flops=2 * slots * rows * width,
     )
-    pack_other = swap(pack, "tensor")
+    pack_other = swap(pack, TE)
     out_rows, pack = lax.optimization_barrier((out_rows, pack))
     out_back = all_to_all(out_rows)
     grad_mixed, grad_att, grad_v, keep, send = call(
@@ -728,7 +680,7 @@
         scalars=1, flops=8 * rows * width * hidden,
     )
     piece = half // count
-    got = swap(send, "dp")
+    got = swap(send, DP)
     early = (keep.astype(F32) + got.astype(F32)).astype(BF)
     early = all_to_all(early.reshape(count, piece, -1))
     part1, keep, send = call(
@@ -743,18 +695,21 @@
         scalars=1, flops=12 * rows * width * hidden,
     )
     late = reduce_dense(ids, keep, send)
-    part1_other = swap(part1, "tensor")
-    w_out_t, grad_v_w, small = call(
+    part1_other = swap(part1, TE)
+    w_out_t, grad_v_w, router_rows, b_row, scale_row, shift_row = call(
         early_end_kernel,
-        [((piece, hidden), F32), ((piece, hidden), F32), ((piece, LANES), F32)],
+        [((piece, hidden), F32), ((piece, hidden), F32), ((experts, piece), F32)]
+        + [((1, piece), F32)] * 3,
         early,
+        scratch=[pltpu.VMEM((LANES, LANES), F32)],
     )
     grad_w_qkv, ln1 = call(
         late_end_kernel,
-        [((3, piece, hidden), F32), ((piece, LANES), F32)],
+        [((3, piece, hidden), F32), ((8, LANES), F32)],
         *late, grad_v_w,
-    )
-    ln1 = ln1 + swap(ln1, "tensor")
+        scratch=[pltpu.VMEM((LANES, LANES), F32)],
+    )
+    ln1 = ln1 + swap(ln1, TE)
     (grad_tokens,) = call(
         norm1_back_kernel,
         [((rows, width), BF)],
@@ -766,43 +721,43 @@
         target, out_back.reshape(slots, width),
         flops=2 * slots * rows * width,
     )
-    out_other = swap(out_part, "tensor")
+    out_other = swap(out_part, TE)
     out = (mixed + (out_part.astype(F32) + out_other.astype(F32))).astype(BF)
     return (
         out,
         grad_tokens,
-        ln1[:, 0],
-        ln1[:, 1],
+        ln1[0, :piece],
+        ln1[1, :piece],
         grad_w_qkv.transpose(1, 0, 2),
         w_out_t.T,
-        small[:, experts],
-        small[:, experts + 1],
-        small[:, experts + 2],
-        small[:, :experts],
+        b_row.reshape(piece),
+        scale_row.reshape(piece),
+        shift_row.reshape(piece),
+        router_rows.T,
         grad_w_in[None],
-        biases[:, :inner],
+        grad_b_in,
         grad_w_exp_out[None],
-        biases[:, inner:],
+        grad_b_exp_out,
     )
 
 
 def solution(mesh):
-    rows = P(("dp", "expert"), None)
-    shard = P(("dp", "expert"))
+    rows = P((DP, EX), None)
+    shard = P((DP, EX))
     placed = (
         rows,
         P(),
         P(),
-        P(None, None, "tensor"),
-        P("tensor", None),
+        P(None, None, TE),
+        P(TE, None),
         P(),
         P(),
         P(),
         P(),
-        P("expert", None, "tensor"),
-        P("expert", "tensor"),
-        P("expert", "tensor", None),
-        P("expert", None),
+        P(EX, None, TE),
+        P(EX, TE),
+        P(EX, TE, None),
+        P(EX, None),
         rows,
         rows,
     )
@@ -815,16 +770,16 @@
             rows,
             shard,
             shard,
-            P(("dp", "expert"), None, "tensor"),
-            P("tensor", ("dp", "expert")),
+            P((DP, EX), None, TE),
+            P(TE, (DP, EX)),
             shard,
             shard,
             shard,
             rows,
-            P("expert", None, "tensor"),
-            P("expert", "tensor"),
-            P("expert", "tensor", None),
-            P("expert", None),
+            P(EX, None, TE),
+            P(EX, TE),
+            P(EX, TE, None),
+            P(EX, None),
         ),
         check_vma=False,
     )

time: 173 us -> 167 us (0.965)
  Pallas kernels: 68.2 us -> 56.2 us
  waiting for transfers between devices: 28.4 us -> 33.6 us
  local copies, waits for them, and re-layouts: 9.46 us -> 4.44 us
  other arithmetic: 4.29 us -> 8.35 us
  matrix products: 3.08 us -> 6.75 us
    pallas_call x13 -> x10, Pallas kernels: 38.4 us -> 32.2 us  [call(): pl.pallas_call(kernel, out_shape=tuple((jax.ShapeDtypeStruct(s, d) for s,...]
    pallas_call x4 -> x3, Pallas kernels: 29.8 us -> 24 us  [the longest x2 14.3 us: weight_grad(): pl.pallas_call(weight_grad_kernel, grid=(rows // tile,), out_shape=[jax.S...]
    dot_general x0 -> x1, matrix products: none -> 3.67 us  [dot32(): return jnp.dot(a, b, preferred_element_type=F32)]
    unnamed x56 -> x42, local copies, waits for them, and re-layouts: 5.98 us -> 2.83 us
    convert_element_type x0 -> x3, other arithmetic: none -> 2.97 us  [half_sum(): return (lax.dynamic_index_in_dim(keep.reshape(pair), which, 1, keepdims=F...]
    ppermute x12 -> x11, waiting for transfers between devices: 11.5 us -> 14.4 us  [swap(): return lax.ppermute(x, axis, [(0, 1), (1, 0)])]
    slice x4 -> x1, local copies, waits for them, and re-layouts: 3.47 us -> 1.09 us  [per_device(): out_rows = gate[:, :1] * (dot32(hidden_act, w_exp_out) + own_bias)]
    ppermute x17, waiting for transfers between devices: 16.9 us -> 19.2 us  [the longest x14 10.7 us: xor_exchange(): outs[k] = lax.ppermute(blocks[k], EX, [(i, i ^ k) for i in range(count)])]
  transfers between devices with their start and end apart: 32 -> 31, of which waited for: 7 -> 8; matrix products, arithmetic and copies ran while one was open for 6% -> 9% of each run, Pallas kernels for 30% -> 25%
where the time goes in v1:
time: 167 us; the launch traced here: 166 us
  starting transfers between devices  56.3 us (34%)
  Pallas kernels  56.2 us (34%)
  waiting for transfers between devices  33.6 us (20%)
  other arithmetic  8.35 us (5%)
  matrix products  6.75 us (4%)
  local copies, waits for them, and re-layouts  4.44 us (3%)
    pallas_call x10, Pallas kernels, call(): pl.pallas_call(kernel, out_shape=tuple((jax.ShapeDtypeStruct(s, d) for s,...  32.2 us
    ppermute x14, starting transfers between devices, xor_exchange(): outs[k] = lax.ppermute(blocks[k], EX, [(i, i ^ k) for i in range(count)])  23.5 us
    all_to_all x3, starting transfers between devices, all_to_all(): return lax.all_to_all(x, EX, split_axis=0, concat_axis=0, tiled=True)  19.2 us
    ppermute x11, waiting for transfers between devices, swap(): return lax.ppermute(x, axis, [(0, 1), (1, 0)])  14.4 us
    pallas_call x2, Pallas kernels, weight_grad(): pl.pallas_call(weight_grad_kernel, grid=(rows // tile,), out_shape=[jax.S...  14.3 us
    ppermute x14, waiting for transfers between devices, xor_exchange(): outs[k] = lax.ppermute(blocks[k], EX, [(i, i ^ k) for i in range(count)])  10.7 us
    pallas_call x1, Pallas kernels, per_device(): pl.pallas_call(functools.partial(expert_kernel, (experts, capacity, cap_p...  9.68 us
    ppermute x3, waiting for transfers between devices, reduce_dense(): got = lax.ppermute(send, EX, [(i, i ^ 1 << bit) for i in range(count)])  8.52 us
  transfers between devices with their start and end apart: 31, of which 8 were waited for; matrix products, arithmetic and copies ran while one was open for 9% of the time, Pallas kernels for 25%

profile of v1, /device:TPU:0, one launch (start us, length us, event | category | flops | bytes accessed | tf_op | source)
XLA Modules:
  0.0 166.4 jit_solution(8293271389705171594)
XLA Ops:
  1.3 2.5 %shard_map.255 = (s32[4,256]{1,0:T(4,128)}, bf16[512,768]{1,0:T(8,128)(2,1)}) custom-call(s32[3]{0:T(128)} %pad_add_fusion.ids_ref, s32[2,197]{1,0:T(2,128)} %bitcast.68, bf16[197,768]{1,0:T(8,128)(2,1)} %cot_ref.3), custom_call_target="tpu_custom_call" | custom-call | flops 154927104 | bytes 304180 | tf_op jit(solution)/shard_map/pallas_call | solution.py:500
  3.8 7.3 %all-to-all-start = ((bf16[8,64,768]{2,1,0:T(8,128)(2,1)}), bf16[8,64,768]{2,1,0:T(8,128)(2,1)S(1)}, u32[]{:S(2)}, u32[]{:S(2)}) async-start(bf16[8,64,768]{2,1,0:T(8,128)(2,1)} %bitcast.63), calls=%async_computation | async-start | bytes 1572864 | tf_op jit(solution)/shard_map/all_to_all | solution.py:523
  11.1 4.3 %shard_map.254 = (bf16[197,768]{1,0:T(8,128)(2,1)}, bf16[197,384]{1,0:T(8,128)(2,1)}, bf16[3,197,384]{2,1,0:T(8,128)(2,1)}, f32[197,128]{1,0:T(8,128)}) custom-call(bf16[197,768]{1,0:T(8,128)(2,1)} %tok_ref.9, f32[768]{0:T(1024)} %scale_ref.9, f32[768]{0:T(1024)} %shift_ref.9, bf16[3,768,384]{2,1,0:T(8,128)(2,1)} %bitcast.55, bf16[384,768]{1,0:T(8,128)(2,1)} %w_out_ref.3), custom_call_target="tpu_custom_call" | custom-call | flops 464781312 | bytes 2668032 | tf_op jit(solution)/shard_map/pallas_call | solution.py:500
  15.3 1.5 collective-permute-start
  16.8 7.4 %collective-permute-done.part2_ref = bf16[197,768]{1,0:T(8,128)(2,1)S(1)} collective-permute-done((bf16[197,768]{1,0:T(8,128)(2,1)}, bf16[197,768]{1,0:T(8,128)(2,1)S(1)}, u32[]{:S(2)}, u32[]{:S(2)}) %collective-permute-start) | collective-permute-done | bytes 302624 | tf_op jit(solution)/shard_map/ppermute | solution.py:512
  24.3 0.7 copy-done.7
  25.0 2.9 %shard_map.256 = (f32[197,768]{1,0:T(8,128)}, f32[8,197]{1,0:T(8,128)}, bf16[64,768]{1,0:T(8,128)(2,1)}, bf16[64,768]{1,0:T(8,128)(2,1)}, bf16[64,768]{1,0:T(8,1...) custom-call(bf16[197,768]{1,0:T(8,128)(2,1)} %tok_ref.9, ...), custom_call_target="tpu_custom_call" | custom-call | flops 154927104 | bytes 934952 | tf_op jit(solution)/shard_map/pallas_call | solution.py:500
  27.9 1.8 %collective-permute-start.1 = (bf16[64,768]{1,0:T(8,128)(2,1)}, bf16[64,768]{1,0:T(8,128)(2,1)S(1)}, u32[]{:S(2)}, u32[]{:S(2)}) collective-permute-start(bf16[64,768]{1,0:T(8,128)(2,1)} %get-tuple-element.70), channel_id=1, source_target_pairs={{0,2},{2,0},{4,6},{6,4},{8,10},{10,8},{12,14},{14,12},{1,3},{3,1},... | collective-permute-start | bytes 294920 | tf_op jit(solution)/shard_map/ppermute | solution.py:518
  29.7 1.5 collective-permute-start.2
  31.5 2.6 %collective-permute-start.4 = (bf16[64,768]{1,0:T(8,128)(2,1)}, bf16[64,768]{1,0:T(8,128)(2,1)S(1)}, u32[]{:S(2)}, u32[]{:S(2)}) collective-permute-start(bf16[64,768]{1,0:T(8,128)(2,1)} %get-tuple-element.73), channel_id=1, source_target_pairs={{0,8},{2,10},{4,12},{6,14},{8,0},{10,2},{12,4},{14,6},{1,9},{3,11}... | collective-permute-start | bytes 294920 | tf_op jit(solution)/shard_map/ppermute | solution.py:518
  34.2 1.5 collective-permute-start.5
  35.6 3.3 %collective-permute-start.6 = (bf16[64,768]{1,0:T(8,128)(2,1)}, bf16[64,768]{1,0:T(8,128)(2,1)}, u32[]{:S(2)}, u32[]{:S(2)}) collective-permute-start(bf16[64,768]{1,0:T(8,128)(2,1)} %get-tuple-element.75), channel_id=1, source_target_pairs={{0,12},{2,14},{4,8},{6,10},{8,4},{10,6},{12,0},{14,2},{1,13},{3,15... | collective-permute-start | bytes 294920 | tf_op jit(solution)/shard_map/ppermute | solution.py:518
  39.2 3.1 %fusion.2.raw_ref = f32[512,1536]{1,0:T(8,128)} fusion(bf16[512,768]{1,0:T(8,128)(2,1)S(1)} %bitcast.60, bf16[1,1536,768]{2,1,0:T(8,128)(2,1)S(1)} %copy-done), kind=kOutput, calls=%fused_computation.2 | convolution fusion | flops 1207959552 | bytes 6291456 | tf_op jit(solution)/shard_map/dot_general | solution.py:49
  42.3 3.5 %collective-permute-done.4.refs_4_ = bf16[64,768]{1,0:T(8,128)(2,1)S(1)} collective-permute-done((bf16[64,768]{1,0:T(8,128)(2,1)}, bf16[64,768]{1,0:T(8,128)(2,1)S(1)}, u32[]{:S(2)}, u32[]{:S(2)}) %collective-permute-start.4) | collective-permute-done | bytes 98336 | tf_op jit(solution)/shard_map/ppermute | solution.py:518
  45.7 3.7 %collective-permute-done.5.refs_5_ = bf16[64,768]{1,0:T(8,128)(2,1)} collective-permute-done((bf16[64,768]{1,0:T(8,128)(2,1)}, bf16[64,768]{1,0:T(8,128)(2,1)}, u32[]{:S(2)}, u32[]{:S(2)}) %collective-permute-start.5) | collective-permute-done | bytes 98336 | tf_op jit(solution)/shard_map/ppermute | solution.py:518
  49.5 9.7 %shard_map.257 = (bf16[512,768]{1,0:T(8,128)(2,1)}, f32[512,128]{1,0:T(8,128)}, bf16[512,1536]{1,0:T(8,128)(2,1)}, bf16[512,1536]{1,0:T(8,128)(2,1)}, bf16[512,7...) custom-call(s32[3]{0:T(128)} %pad_add_fusion.ids_ref, ...), custom_call_target="tpu_custom_call" | custom-call | flops 2415919104 | bytes 12000000 | tf_op jit(solution)/shard_map/pallas_call | solution.py:615
  59.2 3.6 %collective-permute-start.9 = (bf16[64,768]{1,0:T(8,128)(2,1)}, bf16[64,768]{1,0:T(8,128)(2,1)S(1)}, u32[]{:S(2)}, u32[]{:S(2)}) collective-permute-start(bf16[64,768]{1,0:T(8,128)(2,1)} %get-tuple-element.81), channel_id=1, source_target_pairs={{0,4},{2,6},{4,0},{6,2},{8,12},{10,14},{12,8},{14,10},{1,5},{3,7},... | collective-permute-start | bytes 294920 | tf_op jit(solution)/shard_map/ppermute | solution.py:518
  62.8 0.9 collective-permute-start.10
  63.7 2.8 %collective-permute-start.11 = (bf16[64,768]{1,0:T(8,128)(2,1)}, bf16[64,768]{1,0:T(8,128)(2,1)S(1)}, u32[]{:S(2)}, u32[]{:S(2)}) collective-permute-start(bf16[64,768]{1,0:T(8,128)(2,1)} %get-tuple-element.83), channel_id=1, source_target_pairs={{0,8},{2,10},{4,12},{6,14},{8,0},{10,2},{12,4},{14,6},{1,9},{3,11}... | collective-permute-start | bytes 294920 | tf_op jit(solution)/shard_map/ppermute | solution.py:518
  66.6 1.1 slice_reduce_fusion
  67.8 2.3 %collective-permute-start.13 = (bf16[64,768]{1,0:T(8,128)(2,1)}, bf16[64,768]{1,0:T(8,128)(2,1)S(1)}, u32[]{:S(2)}, u32[]{:S(2)}) collective-permute-start(bf16[64,768]{1,0:T(8,128)(2,1)} %get-tuple-element.85), channel_id=1, source_target_pairs={{0,12},{2,14},{4,8},{6,10},{8,4},{10,6},{12,0},{14,2},{1,13},{3,15... | collective-permute-start | bytes 294920 | tf_op jit(solution)/shard_map/ppermute | solution.py:518
  70.1 2.5 %collective-permute-start.14 = (bf16[64,768]{1,0:T(8,128)(2,1)}, bf16[64,768]{1,0:T(8,128)(2,1)S(1)}, u32[]{:S(2)}, u32[]{:S(2)}) collective-permute-start(bf16[64,768]{1,0:T(8,128)(2,1)} %get-tuple-element.86), channel_id=1, source_target_pairs={{0,14},{2,12},{4,10},{6,8},{8,6},{10,4},{12,2},{14,0},{1,15},{3,13... | collective-permute-start | bytes 294920 | tf_op jit(solution)/shard_map/ppermute | solution.py:518
  72.5 3.7 %multiply_convert_fusion = bf16[512,768]{1,0:T(8,128)(2,1)} fusion(f32[768]{0:T(1024)S(1)} %fusion.8, f32[512]{0:T(512)S(1)} %slice_reduce_fusion, bf16[512,1536]{1,0:T(8,128)(2,1)} %get-tuple-element.78.a_ref, bf16[1,1536,768]{2,1,0:T(8,128)(2,1)S(1)} %copy-done), kind=kOutput, calls=%fused_computation.4 | convolution fusion | flops 1209139200 | bytes 4723712 | tf_op jit(solution)/shard_map/dot_general | solution.py:45
  76.4 3.3 %collective-permute-done.12.refs_5_ = bf16[64,768]{1,0:T(8,128)(2,1)S(1)} collective-permute-done((bf16[64,768]{1,0:T(8,128)(2,1)}, bf16[64,768]{1,0:T(8,128)(2,1)S(1)}, u32[]{:S(2)}, u32[]{:S(2)}) %collective-permute-start.12) | collective-permute-done | bytes 98336 | tf_op jit(solution)/shard_map/ppermute | solution.py:518
  80.5 2.4 %shard_map.258.pack_ref = bf16[224,768]{1,0:T(8,128)(2,1)} custom-call(s32[4,256]{1,0:T(4,128)} %get-tuple-element.66.target_ref, bf16[64,768]{1,0:T(8,128)(2,1)} %get-tuple-element.79.refs_0_, bf16[64,768]{1,0:T(8,128)(2,1)} %copy-done.8, bf16[64,768]{1,0:T(8,128)(2,1)} %copy-done.9, bf16[64,768]{1,0:T(8,128)(2,1)} %copy-done.10, ...), custom_call_target="tpu_custom_call" | custom-call | flops 154927104 | bytes 790528 | tf_op jit(solution)/shard_map/pallas_call | solution.py:500
  82.9 6.3 %all-to-all-start.1 = ((bf16[8,64,768]{2,1,0:T(8,128)(2,1)}), bf16[8,64,768]{2,1,0:T(8,128)(2,1)S(1)}, u32[]{:S(2)}, u32[]{:S(2)}) async-start(bf16[8,64,768]{2,1,0:T(8,128)(2,1)} %bitcast.62), calls=%async_computation.1 | async-start | bytes 1572864 | tf_op jit(solution)/shard_map/all_to_all | solution.py:523
  89.2 1.5 collective-permute-start.16
  90.7 6.4 %collective-permute-done.16.pack2_ref = bf16[224,768]{1,0:T(8,128)(2,1)S(1)} collective-permute-done((bf16[224,768]{1,0:T(8,128)(2,1)S(1)}, bf16[224,768]{1,0:T(8,128)(2,1)S(1)}, u32[]{:S(2)}, u32[]{:S(2)}) %collective-permute-start.16) | collective-permute-done | bytes 344096 | tf_op jit(solution)/shard_map/ppermute | solution.py:512
  97.1 0.7 copy-done.6
  97.8 5.3 %shard_map.260 = (f32[197,768]{1,0:T(8,128)}, bf16[197,384]{1,0:T(8,128)(2,1)}, bf16[197,384]{1,0:T(8,128)(2,1)}, bf16[384,896]{1,0:T(8,128)(2,1)}, bf16[384,896]{1,0:T(8,128)(2,1)}) custom-call(s32[3]{0:T(128)} %pad_add_fusion.ids_ref, bf16[224,768]{1,0:T(8,128)(2,1)} %shard_map.258.pack_ref, bf16[224,768]{1,0:T(8,128)(2,1)} %copy-done.6, ...), custom_call_target="tpu_custom_call" | custom-call | flops 464781312 | bytes 3226836 | tf_op jit(solution)/shard_map/pallas_call | solution.py:500
  103.7 6.4 %shard_map.261 = (bf16[197,768]{1,0:T(8,128)(2,1)}, bf16[384,896]{1,0:T(8,128)(2,1)}, bf16[384,896]{1,0:T(8,128)(2,1)}) custom-call(s32[3]{0:T(128)} %pad_add_fusion.ids_ref, bf16[197,384]{1,0:T(8,128)(2,1)} %get-tuple-element.93.grad_att_ref, bf16[197,384]{1,0:T(8,128)(2,1)} %get-tuple-element.94.grad_v_ref, ...), custom_call_target="tpu_custom_call" | custom-call | flops 697171968 | bytes 2935564 | tf_op jit(solution)/shard_map/pallas_call | solution.py:500
  110.7 1.5 collective-permute-start.17
  112.2 2.3 %add_convert_fusion = bf16[384,896]{1,0:T(8,128)(2,1)} fusion(bf16[384,896]{1,0:T(8,128)(2,1)} %collective-permute-done.22, bf16[384,896]{1,0:T(8,128)(2,1)} %get-tuple-element.99), kind=kLoop, calls=%fused_computation.5 | loop fusion | flops 1376256 | bytes 2064384 | tf_op jit(solution)/shard_map/convert_element_type | solution.py:684
  114.5 5.6 %all-to-all-start.2 = ((bf16[8,48,896]{2,1,0:T(8,128)(2,1)}), bf16[8,48,896]{2,1,0:T(8,128)(2,1)}, u32[]{:S(2)}, u32[]{:S(2)}) async-start(bf16[8,48,896]{2,1,0:T(8,128)(2,1)} %bitcast.58), calls=%async_computation.2 | async-start | bytes 1376256 | tf_op jit(solution)/shard_map/all_to_all | solution.py:523
  120.1 2.2 %add_convert_fusion.2 = (bf16[4,1,48,896]{3,2,0,1:T(8,128)(2,1)S(1)}, bf16[4,48,896]{2,1,0:T(8,128)(2,1)}) fusion(bf16[4,2,48,896]{3,2,1,0:T(8,128)(2,1)} %bitcast.13, s32[]{:T(128)S(6)} %select_n.37, bf16[4,2,48,896]{3,2,1,0:T(8,128)(2,1)} %bitcast.64, s32[]{:T(128)S(6)} %select_n.39), kind=kLoop, calls=%fused_computation.7 | loop fusion | flops 1376256 | bytes 2064392 | tf_op jit(solution)/shard_map/convert_element_type | solution.py:542
  122.3 2.0 %collective-permute-start.19 = (bf16[4,48,896]{2,1,0:T(8,128)(2,1)}, bf16[4,48,896]{2,1,0:T(8,128)(2,1)S(1)}, u32[]{:S(2)}, u32[]{:S(2)}) collective-permute-start(bf16[4,48,896]{2,1,0:T(8,128)(2,1)} %get-tuple-element.117), channel_id=1, source_target_pairs={{0,2},{2,0},{4,6},{6,4},{8,10},{10,8},{12,14},{14,12},{1,3},{3,1},... | collective-permute-start | bytes 1032200 | tf_op jit(solution)/shard_map/ppermute | solution.py:545
  124.3 2.6 %shard_map.262 = bf16[197,768]{1,0:T(8,128)(2,1)} custom-call(bf16[197,768]{1,0:T(8,128)(2,1)} %get-tuple-element.95.part_ref, bf16[197,768]{1,0:T(8,128)(2,1)} %collective-permute-done.17.part2_ref, bf16[197,768]{1,0:T(8,128)(2,1)} %tok_ref.9, f32[768]{0:T(1024)} %scale_ref.9, f32[768]{0:T(1024)} %shift_ref.9, f32[197,768]{1,0:T(8,128)} %get-tuple-element.96.grad_ref), custom_call_target="tpu_custom_call" | custom-call | bytes 1519104 | tf_op jit(solution)/shard_map/pallas_call | solution.py:500
  126.9 2.3 %shard_map.259 = bf16[197,768]{1,0:T(8,128)(2,1)} custom-call(s32[4,256]{1,0:T(4,128)} %get-tuple-element.66.target_ref, bf16[512,768]{1,0:T(8,128)(2,1)} %bitcast.57), custom_call_target="tpu_custom_call" | custom-call | flops 154927104 | bytes 790528 | tf_op jit(solution)/shard_map/pallas_call | solution.py:500
  129.2 8.5 %collective-permute-done.19 = bf16[4,48,896]{2,1,0:T(8,128)(2,1)S(1)} collective-permute-done((bf16[4,48,896]{2,1,0:T(8,128)(2,1)}, bf16[4,48,896]{2,1,0:T(8,128)(2,1)S(1)}, u32[]{:S(2)}, u32[]{:S(2)}) %collective-permute-start.19) | collective-permute-done | bytes 344096 | tf_op jit(solution)/shard_map/ppermute | solution.py:545
  138.4 1.5 collective-permute-start.20
  139.9 7.3 %shard_map.265 = (f32[768,1536]{1,0:T(8,128)}, f32[1,1536]{1,0:T(1,128)}) custom-call(s32[3]{0:T(128)} %pad_add_fusion.ids_ref, bf16[512,768]{1,0:T(8,128)(2,1)} %get-tuple-element.109.a_ref, bf16[512,768]{1,0:T(8,128)(2,1)} %collective-permute-done.24.a2_ref, bf16[512,1536]{1,0:T(8,128)(2,1)} %get-tuple-element.110.b_ref, ...), custom_call_target="tpu_custom_call" | custom-call | flops 2415919104 | bytes 9000000 | tf_op jit(solution)/shard_map/pallas_call | solution.py:475
  147.9 2.4 %collective-permute-start.21 = (bf16[1,48,896]{2,1,0:T(8,128)(2,1)S(1)}, bf16[1,48,896]{2,1,0:T(8,128)(2,1)S(1)}, u32[]{:S(2)}, u32[]{:S(2)}) collective-permute-start(bf16[1,48,896]{2,1,0:T(8,128)(2,1)S(1)} %get-tuple-element.120), channel_id=1, source_target_pairs={{0,8},{2,10},{4,12},{6,14},{8,0},{10,2},{12,4},{14,6},{1,9},{3,11}... | collective-permute-start | bytes 258056 | tf_op jit(solution)/shard_map/ppermute | solution.py:545
  150.3 7.0 %shard_map.266 = (f32[1536,768]{1,0:T(8,128)}, f32[1,768]{1,0:T(1,128)}) custom-call(s32[3]{0:T(128)} %pad_add_fusion.ids_ref, bf16[512,1536]{1,0:T(8,128)(2,1)} %get-tuple-element.78.a_ref, bf16[512,1536]{1,0:T(8,128)(2,1)} %collective-permute-done.26.a2_ref, bf16[512,768]{1,0:T(8,128)(2,1)} %get-tuple-element.113.b_ref, ...), custom_call_target="tpu_custom_call" | custom-call | flops 2415919104 | bytes 9000000 | tf_op jit(solution)/shard_map/pallas_call | solution.py:475
  157.3 1.8 %shard_map.263 = (f32[48,384]{1,0:T(8,128)}, f32[48,384]{1,0:T(8,128)}, f32[8,48]{1,0:T(8,128)}, f32[1,48]{1,0:T(1,128)}, f32[1,48]{1,0:T(1,128)}, /*index=5*/f32[1,48]{1,0:T(1,128)}) custom-call(bf16[8,48,896]{2,1,0:T(8,128)(2,1)} %all-to-all-done.2.part_ref), custom_call_target="tpu_custom_call" | custom-call | bytes 688128 | tf_op jit(solution)/shard_map/pallas_call | solution.py:500
  159.7 1.7 %shard_map.264 = (f32[3,48,384]{2,1,0:T(8,128)}, f32[8,128]{1,0:T(8,128)}) custom-call(bf16[1,48,896]{2,1,0:T(8,128)(2,1)} %get-tuple-element.121.kept_ref, bf16[1,48,896]{2,1,0:T(8,128)(2,1)} %copy-done.15, f32[48,384]{1,0:T(8,128)} %get-tuple-element.101.v_ref), custom_call_target="tpu_custom_call" | custom-call | bytes 245760 | tf_op jit(solution)/shard_map/pallas_call | solution.py:500
  161.4 1.4 collective-permute-start.23
  162.9 1.8 %add_convert_fusion.3 = bf16[197,768]{1,0:T(8,128)(2,1)} fusion(f32[197,768]{1,0:T(8,128)S(1)} %copy-done.2, bf16[197,768]{1,0:T(8,128)(2,1)} %collective-permute-done.15, bf16[197,768]{1,0:T(8,128)(2,1)S(1)} %copy-done.4), kind=kLoop, calls=%fused_computation.8 | loop fusion | flops 756480 | bytes 1512960 | tf_op jit(solution)/shard_map/convert_element_type | solution.py:725
  165.2 0.7 add.97
  (81 shorter events, 6.6 us)
Async XLA Ops:
  0.6 38.5 %copy-start = (bf16[1,1536,768]{2,1,0:T(8,128)(2,1)S(1)}, bf16[1,1536,768]{2,1,0:T(8,128)(2,1)}, u32[]{:S(2)}) copy-start(bf16[1,1536,768]{2,1,0:T(8,128)(2,1)} %param.26) | copy-start | bytes 7077892
  3.8 35.4 %all-to-all-start = ((bf16[8,64,768]{2,1,0:T(8,128)(2,1)}), bf16[8,64,768]{2,1,0:T(8,128)(2,1)S(1)}, u32[]{:S(2)}, u32[]{:S(2)}) async-start(bf16[8,64,768]{2,1,0:T(8,128)(2,1)} %bitcast.63), calls=%async_computation | async-start | bytes 1572864 | tf_op jit(solution)/shard_map/all_to_all | solution.py:523
  11.1 20.1 %copy-start.16 = (f32[1,768]{1,0:T(1,128)S(1)}, f32[1,768]{1,0:T(1,128)}, u32[]{:S(2)}) copy-start(f32[1,768]{1,0:T(1,128)} %bias2_ref.1) | copy-start | bytes 9220
  15.3 8.9 %collective-permute-start = (bf16[197,768]{1,0:T(8,128)(2,1)}, bf16[197,768]{1,0:T(8,128)(2,1)S(1)}, u32[]{:S(2)}, u32[]{:S(2)}) collective-permute-start(bf16[197,768]{1,0:T(8,128)(2,1)} %get-tuple-element.65.part_ref), channel_id=1, source_target_pairs={{0,1},{1,0},{2,3},{3,2},{4,5},{5,4},{6,7},{7,6},{8,9},{9,8},{10,11... | collective-permute-start | bytes 907784 | tf_op jit(solution)/shard_map/ppermute | solution.py:512
  24.3 0.7 copy-start.7
  27.9 7.7 %collective-permute-start.1 = (bf16[64,768]{1,0:T(8,128)(2,1)}, bf16[64,768]{1,0:T(8,128)(2,1)S(1)}, u32[]{:S(2)}, u32[]{:S(2)}) collective-permute-start(bf16[64,768]{1,0:T(8,128)(2,1)} %get-tuple-element.70), channel_id=1, source_target_pairs={{0,2},{2,0},{4,6},{6,4},{8,10},{10,8},{12,14},{14,12},{1,3},{3,1},... | collective-permute-start | bytes 294920 | tf_op jit(solution)/shard_map/ppermute | solution.py:518
  29.7 9.2 %collective-permute-start.2 = (bf16[64,768]{1,0:T(8,128)(2,1)}, bf16[64,768]{1,0:T(8,128)(2,1)S(1)}, u32[]{:S(2)}, u32[]{:S(2)}) collective-permute-start(bf16[64,768]{1,0:T(8,128)(2,1)} %get-tuple-element.71), channel_id=1, source_target_pairs={{0,4},{2,6},{4,0},{6,2},{8,12},{10,14},{12,8},{14,10},{1,5},{3,7},... | collective-permute-start | bytes 294920 | tf_op jit(solution)/shard_map/ppermute | solution.py:518
  31.2 11.1 %collective-permute-start.3 = (bf16[64,768]{1,0:T(8,128)(2,1)}, bf16[64,768]{1,0:T(8,128)(2,1)S(1)}, u32[]{:S(2)}, u32[]{:S(2)}) collective-permute-start(bf16[64,768]{1,0:T(8,128)(2,1)} %get-tuple-element.72), channel_id=1, source_target_pairs={{0,6},{2,4},{4,2},{6,0},{8,14},{10,12},{12,10},{14,8},{1,7},{3,5},... | collective-permute-start | bytes 294920 | tf_op jit(solution)/shard_map/ppermute | solution.py:518
  31.5 14.2 %collective-permute-start.4 = (bf16[64,768]{1,0:T(8,128)(2,1)}, bf16[64,768]{1,0:T(8,128)(2,1)S(1)}, u32[]{:S(2)}, u32[]{:S(2)}) collective-permute-start(bf16[64,768]{1,0:T(8,128)(2,1)} %get-tuple-element.73), channel_id=1, source_target_pairs={{0,8},{2,10},{4,12},{6,14},{8,0},{10,2},{12,4},{14,6},{1,9},{3,11}... | collective-permute-start | bytes 294920 | tf_op jit(solution)/shard_map/ppermute | solution.py:518
  34.2 15.3 %collective-permute-start.5 = (bf16[64,768]{1,0:T(8,128)(2,1)}, bf16[64,768]{1,0:T(8,128)(2,1)}, u32[]{:S(2)}, u32[]{:S(2)}) collective-permute-start(bf16[64,768]{1,0:T(8,128)(2,1)} %get-tuple-element.74), channel_id=1, source_target_pairs={{0,10},{2,8},{4,14},{6,12},{8,2},{10,0},{12,6},{14,4},{1,11},{3,9}... | collective-permute-start | bytes 294920 | tf_op jit(solution)/shard_map/ppermute | solution.py:518
  35.6 6.6 %copy-start.17 = (bf16[64,768]{1,0:T(8,128)(2,1)}, bf16[64,768]{1,0:T(8,128)(2,1)S(1)}, u32[]{:S(2)}) copy-start(bf16[64,768]{1,0:T(8,128)(2,1)S(1)} %collective-permute-done.1.refs_1_) | copy-start | bytes 294916
  35.6 13.8 %collective-permute-start.6 = (bf16[64,768]{1,0:T(8,128)(2,1)}, bf16[64,768]{1,0:T(8,128)(2,1)}, u32[]{:S(2)}, u32[]{:S(2)}) collective-permute-start(bf16[64,768]{1,0:T(8,128)(2,1)} %get-tuple-element.75), channel_id=1, source_target_pairs={{0,12},{2,14},{4,8},{6,10},{8,4},{10,6},{12,0},{14,2},{1,13},{3,15... | collective-permute-start | bytes 294920 | tf_op jit(solution)/shard_map/ppermute | solution.py:518
  38.9 3.4 %copy-start.18 = (bf16[64,768]{1,0:T(8,128)(2,1)}, bf16[64,768]{1,0:T(8,128)(2,1)S(1)}, u32[]{:S(2)}) copy-start(bf16[64,768]{1,0:T(8,128)(2,1)S(1)} %collective-permute-done.2.refs_2_) | copy-start | bytes 294916
  38.9 10.6 %collective-permute-start.7 = (bf16[64,768]{1,0:T(8,128)(2,1)}, bf16[64,768]{1,0:T(8,128)(2,1)}, u32[]{:S(2)}, u32[]{:S(2)}) collective-permute-start(bf16[64,768]{1,0:T(8,128)(2,1)} %get-tuple-element.76), channel_id=1, source_target_pairs={{0,14},{2,12},{4,10},{6,8},{8,6},{10,4},{12,2},{14,0},{1,15},{3,13... | collective-permute-start | bytes 294920 | tf_op jit(solution)/shard_map/ppermute | solution.py:518
  39.2 3.1 %copy-start.5 = (bf16[8,64,768]{2,1,0:T(8,128)(2,1)}, bf16[8,64,768]{2,1,0:T(8,128)(2,1)S(1)}, u32[]{:S(2)}) copy-start(bf16[8,64,768]{2,1,0:T(8,128)(2,1)S(1)} %all-to-all-done) | copy-start | bytes 2359300
  42.3 7.2 %copy-start.19 = (bf16[64,768]{1,0:T(8,128)(2,1)}, bf16[64,768]{1,0:T(8,128)(2,1)S(1)}, u32[]{:S(2)}) copy-start(bf16[64,768]{1,0:T(8,128)(2,1)S(1)} %collective-permute-done.3.refs_3_) | copy-start | bytes 294916
  45.7 3.7 %copy-start.20 = (bf16[64,768]{1,0:T(8,128)(2,1)}, bf16[64,768]{1,0:T(8,128)(2,1)S(1)}, u32[]{:S(2)}) copy-start(bf16[64,768]{1,0:T(8,128)(2,1)S(1)} %collective-permute-done.4.refs_4_) | copy-start | bytes 294916
  59.2 8.6 %collective-permute-start.8 = (bf16[64,768]{1,0:T(8,128)(2,1)}, bf16[64,768]{1,0:T(8,128)(2,1)S(1)}, u32[]{:S(2)}, u32[]{:S(2)}) collective-permute-start(bf16[64,768]{1,0:T(8,128)(2,1)} %get-tuple-element.80), channel_id=1, source_target_pairs={{0,2},{2,0},{4,6},{6,4},{8,10},{10,8},{12,14},{14,12},{1,3},{3,1},... | collective-permute-start | bytes 294920 | tf_op jit(solution)/shard_map/ppermute | solution.py:518
  59.2 10.8 %collective-permute-start.9 = (bf16[64,768]{1,0:T(8,128)(2,1)}, bf16[64,768]{1,0:T(8,128)(2,1)S(1)}, u32[]{:S(2)}, u32[]{:S(2)}) collective-permute-start(bf16[64,768]{1,0:T(8,128)(2,1)} %get-tuple-element.81), channel_id=1, source_target_pairs={{0,4},{2,6},{4,0},{6,2},{8,12},{10,14},{12,8},{14,10},{1,5},{3,7},... | collective-permute-start | bytes 294920 | tf_op jit(solution)/shard_map/ppermute | solution.py:518
  62.8 13.4 %collective-permute-start.10 = (bf16[64,768]{1,0:T(8,128)(2,1)}, bf16[64,768]{1,0:T(8,128)(2,1)S(1)}, u32[]{:S(2)}, u32[]{:S(2)}) collective-permute-start(bf16[64,768]{1,0:T(8,128)(2,1)} %get-tuple-element.82), channel_id=1, source_target_pairs={{0,6},{2,4},{4,2},{6,0},{8,14},{10,12},{12,10},{14,8},{1,7},{3,5},... | collective-permute-start | bytes 294920 | tf_op jit(solution)/shard_map/ppermute | solution.py:518
  63.7 12.7 %collective-permute-start.11 = (bf16[64,768]{1,0:T(8,128)(2,1)}, bf16[64,768]{1,0:T(8,128)(2,1)S(1)}, u32[]{:S(2)}, u32[]{:S(2)}) collective-permute-start(bf16[64,768]{1,0:T(8,128)(2,1)} %get-tuple-element.83), channel_id=1, source_target_pairs={{0,8},{2,10},{4,12},{6,14},{8,0},{10,2},{12,4},{14,6},{1,9},{3,11}... | collective-permute-start | bytes 294920 | tf_op jit(solution)/shard_map/ppermute | solution.py:518
  66.5 13.2 %collective-permute-start.12 = (bf16[64,768]{1,0:T(8,128)(2,1)}, bf16[64,768]{1,0:T(8,128)(2,1)S(1)}, u32[]{:S(2)}, u32[]{:S(2)}) collective-permute-start(bf16[64,768]{1,0:T(8,128)(2,1)} %get-tuple-element.84), channel_id=1, source_target_pairs={{0,10},{2,8},{4,14},{6,12},{8,2},{10,0},{12,6},{14,4},{1,11},{3,9}... | collective-permute-start | bytes 294920 | tf_op jit(solution)/shard_map/ppermute | solution.py:518
  67.8 8.5 %copy-start.8 = (bf16[64,768]{1,0:T(8,128)(2,1)}, bf16[64,768]{1,0:T(8,128)(2,1)S(1)}, u32[]{:S(2)}) copy-start(bf16[64,768]{1,0:T(8,128)(2,1)S(1)} %collective-permute-done.8.refs_1_) | copy-start | bytes 294916
  67.8 12.0 %collective-permute-start.13 = (bf16[64,768]{1,0:T(8,128)(2,1)}, bf16[64,768]{1,0:T(8,128)(2,1)S(1)}, u32[]{:S(2)}, u32[]{:S(2)}) collective-permute-start(bf16[64,768]{1,0:T(8,128)(2,1)} %get-tuple-element.85), channel_id=1, source_target_pairs={{0,12},{2,14},{4,8},{6,10},{8,4},{10,6},{12,0},{14,2},{1,13},{3,15... | collective-permute-start | bytes 294920 | tf_op jit(solution)/shard_map/ppermute | solution.py:518
  70.1 6.2 %copy-start.9 = (bf16[64,768]{1,0:T(8,128)(2,1)}, bf16[64,768]{1,0:T(8,128)(2,1)S(1)}, u32[]{:S(2)}) copy-start(bf16[64,768]{1,0:T(8,128)(2,1)S(1)} %collective-permute-done.9.refs_2_) | copy-start | bytes 294916
  70.1 9.7 %collective-permute-start.14 = (bf16[64,768]{1,0:T(8,128)(2,1)}, bf16[64,768]{1,0:T(8,128)(2,1)S(1)}, u32[]{:S(2)}, u32[]{:S(2)}) collective-permute-start(bf16[64,768]{1,0:T(8,128)(2,1)} %get-tuple-element.86), channel_id=1, source_target_pairs={{0,14},{2,12},{4,10},{6,8},{8,6},{10,4},{12,2},{14,0},{1,15},{3,13... | collective-permute-start | bytes 294920 | tf_op jit(solution)/shard_map/ppermute | solution.py:518
  76.2 3.5 %copy-start.10 = (bf16[64,768]{1,0:T(8,128)(2,1)}, bf16[64,768]{1,0:T(8,128)(2,1)S(1)}, u32[]{:S(2)}) copy-start(bf16[64,768]{1,0:T(8,128)(2,1)S(1)} %collective-permute-done.10.refs_3_) | copy-start | bytes 294916
  76.4 3.4 %copy-start.11 = (bf16[64,768]{1,0:T(8,128)(2,1)}, bf16[64,768]{1,0:T(8,128)(2,1)S(1)}, u32[]{:S(2)}) copy-start(bf16[64,768]{1,0:T(8,128)(2,1)S(1)} %collective-permute-done.11.refs_4_) | copy-start | bytes 294916
  82.9 6.3 %copy-start.3 = (bf16[224,768]{1,0:T(8,128)(2,1)S(1)}, bf16[224,768]{1,0:T(8,128)(2,1)}, u32[]{:S(2)}) copy-start(bf16[224,768]{1,0:T(8,128)(2,1)} %shard_map.258.pack_ref) | copy-start | bytes 1032196
  82.9 31.6 %all-to-all-start.1 = ((bf16[8,64,768]{2,1,0:T(8,128)(2,1)}), bf16[8,64,768]{2,1,0:T(8,128)(2,1)S(1)}, u32[]{:S(2)}, u32[]{:S(2)}) async-start(bf16[8,64,768]{2,1,0:T(8,128)(2,1)} %bitcast.62), calls=%async_computation.1 | async-start | bytes 1572864 | tf_op jit(solution)/shard_map/all_to_all | solution.py:523
  89.2 7.9 %collective-permute-start.16 = (bf16[224,768]{1,0:T(8,128)(2,1)S(1)}, bf16[224,768]{1,0:T(8,128)(2,1)S(1)}, u32[]{:S(2)}, u32[]{:S(2)}) collective-permute-start(bf16[224,768]{1,0:T(8,128)(2,1)S(1)} %copy-done.3), channel_id=1, source_target_pairs={{0,1},{1,0},{2,3},{3,2},{4,5},{5,4},{6,7},{7,6},{8,9},{9,8},{10,11... | collective-permute-start | bytes 1032200 | tf_op jit(solution)/shard_map/ppermute | solution.py:512
  97.1 0.7 copy-start.6
  103.2 7.5 %collective-permute-start.22 = (bf16[384,896]{1,0:T(8,128)(2,1)}, bf16[384,896]{1,0:T(8,128)(2,1)}, u32[]{:S(2)}, u32[]{:S(2)}) collective-permute-start(bf16[384,896]{1,0:T(8,128)(2,1)} %get-tuple-element.100), channel_id=1, source_target_pairs={{0,16},{16,0},{1,17},{17,1},{2,18},{18,2},{3,19},{19,3},{4,20},{20... | collective-permute-start | bytes 2064392 | tf_op jit(solution)/shard_map/ppermute | solution.py:512
  103.2 36.7 %collective-permute-start.25 = (bf16[512,1536]{1,0:T(8,128)(2,1)}, bf16[512,1536]{1,0:T(8,128)(2,1)}, u32[]{:S(2)}, u32[]{:S(2)}) collective-permute-start(bf16[512,1536]{1,0:T(8,128)(2,1)} %get-tuple-element.110.b_ref), channel_id=1, source_target_pairs={{0,16},{16,0},{1,17},{17,1},{2,18},{18,2},{3,19},{19,3},{4,20},{20... | collective-permute-start | bytes 4718600 | tf_op jit(solution)/shard_map/ppermute | solution.py:512
  110.1 10.0 %collective-permute-start.18 = (bf16[384,896]{1,0:T(8,128)(2,1)}, bf16[384,896]{1,0:T(8,128)(2,1)}, u32[]{:S(2)}, u32[]{:S(2)}) collective-permute-start(bf16[384,896]{1,0:T(8,128)(2,1)} %get-tuple-element.98), channel_id=1, source_target_pairs={{0,16},{16,0},{1,17},{17,1},{2,18},{18,2},{3,19},{19,3},{4,20},{20... | collective-permute-start | bytes 2064392 | tf_op jit(solution)/shard_map/ppermute | solution.py:512
  110.2 40.1 %collective-permute-start.26 = (bf16[512,1536]{1,0:T(8,128)(2,1)}, bf16[512,1536]{1,0:T(8,128)(2,1)}, u32[]{:S(2)}, u32[]{:S(2)}) collective-permute-start(bf16[512,1536]{1,0:T(8,128)(2,1)} %get-tuple-element.78.a_ref), channel_id=1, source_target_pairs={{0,16},{16,0},{1,17},{17,1},{2,18},{18,2},{3,19},{19,3},{4,20},{20... | collective-permute-start | bytes 4718600 | tf_op jit(solution)/shard_map/ppermute | solution.py:512
  110.6 27.8 %collective-permute-start.24 = (bf16[512,768]{1,0:T(8,128)(2,1)}, bf16[512,768]{1,0:T(8,128)(2,1)}, u32[]{:S(2)}, u32[]{:S(2)}) collective-permute-start(bf16[512,768]{1,0:T(8,128)(2,1)} %get-tuple-element.109.a_ref), channel_id=1, source_target_pairs={{0,16},{16,0},{1,17},{17,1},{2,18},{18,2},{3,19},{19,3},{4,20},{20... | collective-permute-start | bytes 2359304 | tf_op jit(solution)/shard_map/ppermute | solution.py:512
  110.7 13.6 %collective-permute-start.17 = (bf16[197,768]{1,0:T(8,128)(2,1)}, bf16[197,768]{1,0:T(8,128)(2,1)}, u32[]{:S(2)}, u32[]{:S(2)}) collective-permute-start(bf16[197,768]{1,0:T(8,128)(2,1)} %get-tuple-element.95.part_ref), channel_id=1, source_target_pairs={{0,1},{1,0},{2,3},{3,2},{4,5},{5,4},{6,7},{7,6},{8,9},{9,8},{10,11... | collective-permute-start | bytes 907784 | tf_op jit(solution)/shard_map/ppermute | solution.py:512
  114.5 7.8 %copy-start.1 = (bf16[8,64,768]{2,1,0:T(8,128)(2,1)}, bf16[8,64,768]{2,1,0:T(8,128)(2,1)S(1)}, u32[]{:S(2)}) copy-start(bf16[8,64,768]{2,1,0:T(8,128)(2,1)S(1)} %all-to-all-done.1) | copy-start | bytes 2359300
  114.5 42.8 %all-to-all-start.2 = ((bf16[8,48,896]{2,1,0:T(8,128)(2,1)}), bf16[8,48,896]{2,1,0:T(8,128)(2,1)}, u32[]{:S(2)}, u32[]{:S(2)}) async-start(bf16[8,48,896]{2,1,0:T(8,128)(2,1)} %bitcast.58), calls=%async_computation.2 | async-start | bytes 1376256 | tf_op jit(solution)/shard_map/all_to_all | solution.py:523
  122.3 15.4 %collective-permute-start.19 = (bf16[4,48,896]{2,1,0:T(8,128)(2,1)}, bf16[4,48,896]{2,1,0:T(8,128)(2,1)S(1)}, u32[]{:S(2)}, u32[]{:S(2)}) collective-permute-start(bf16[4,48,896]{2,1,0:T(8,128)(2,1)} %get-tuple-element.117), channel_id=1, source_target_pairs={{0,2},{2,0},{4,6},{6,4},{8,10},{10,8},{12,14},{14,12},{1,3},{3,1},... | collective-permute-start | bytes 1032200 | tf_op jit(solution)/shard_map/ppermute | solution.py:545
  124.3 25.9 %collective-permute-start.27 = (bf16[512,768]{1,0:T(8,128)(2,1)}, bf16[512,768]{1,0:T(8,128)(2,1)}, u32[]{:S(2)}, u32[]{:S(2)}) collective-permute-start(bf16[512,768]{1,0:T(8,128)(2,1)} %get-tuple-element.113.b_ref), channel_id=1, source_target_pairs={{0,16},{16,0},{1,17},{17,1},{2,18},{18,2},{3,19},{19,3},{4,20},{20... | collective-permute-start | bytes 2359304 | tf_op jit(solution)/shard_map/ppermute | solution.py:512
  137.7 25.1 %collective-permute-start.15 = (bf16[197,768]{1,0:T(8,128)(2,1)}, bf16[197,768]{1,0:T(8,128)(2,1)}, u32[]{:S(2)}, u32[]{:S(2)}) collective-permute-start(bf16[197,768]{1,0:T(8,128)(2,1)} %shard_map.259), channel_id=1, source_target_pairs={{0,1},{1,0},{2,3},{3,2},{4,5},{5,4},{6,7},{7,6},{8,9},{9,8},{10,11... | collective-permute-start | bytes 907784 | tf_op jit(solution)/shard_map/ppermute | solution.py:512
  138.4 8.8 %collective-permute-start.20 = (bf16[2,48,896]{2,1,0:T(8,128)(2,1)S(1)}, bf16[2,48,896]{2,1,0:T(8,128)(2,1)S(1)}, u32[]{:S(2)}, u32[]{:S(2)}) collective-permute-start(bf16[2,48,896]{2,1,0:T(8,128)(2,1)S(1)} %get-tuple-element.119), channel_id=1, source_target_pairs={{0,4},{2,6},{4,0},{6,2},{8,12},{10,14},{12,8},{14,10},{1,5},{3,7},... | collective-permute-start | bytes 516104 | tf_op jit(solution)/shard_map/ppermute | solution.py:545
  147.9 15.0 %copy-start.2 = (f32[197,768]{1,0:T(8,128)S(1)}, f32[197,768]{1,0:T(8,128)}, u32[]{:S(2)}) copy-start(f32[197,768]{1,0:T(8,128)} %get-tuple-element.67.mixed_ref) | copy-start | bytes 1815556
  147.9 15.0 %copy-start.4 = (bf16[197,768]{1,0:T(8,128)(2,1)S(1)}, bf16[197,768]{1,0:T(8,128)(2,1)}, u32[]{:S(2)}) copy-start(bf16[197,768]{1,0:T(8,128)(2,1)} %shard_map.259) | copy-start | bytes 907780
  147.9 11.2 %collective-permute-start.21 = (bf16[1,48,896]{2,1,0:T(8,128)(2,1)S(1)}, bf16[1,48,896]{2,1,0:T(8,128)(2,1)S(1)}, u32[]{:S(2)}, u32[]{:S(2)}) collective-permute-start(bf16[1,48,896]{2,1,0:T(8,128)(2,1)S(1)} %get-tuple-element.120), channel_id=1, source_target_pairs={{0,8},{2,10},{4,12},{6,14},{8,0},{10,2},{12,4},{14,6},{1,9},{3,11}... | collective-permute-start | bytes 258056 | tf_op jit(solution)/shard_map/ppermute | solution.py:545
  161.4 3.8 %collective-permute-start.23 = (f32[8,128]{1,0:T(8,128)}, f32[8,128]{1,0:T(8,128)S(1)}, u32[]{:S(2)}, u32[]{:S(2)}) collective-permute-start(f32[8,128]{1,0:T(8,128)} %get-tuple-element.102), channel_id=1, source_target_pairs={{0,1},{1,0},{2,3},{3,2},{4,5},{5,4},{6,7},{7,6},{8,9},{9,8},{10,11... | collective-permute-start | bytes 12296 | tf_op jit(solution)/shard_map/ppermute | solution.py:512
  (4 other events, 2.6 us)
